TPU v7x, 32 devices: a whole 2x2x4 slice. The times are simulated.
32 devices in a mesh: fsdp: 2 (over x), ctx: 4 (over z), tp: 4 (over y, core).
Axes of the slice: x: 2, y: 2, z: 4, core: 2. Of those that a mesh axis runs over, the one named last changes fastest.
Arguments:
- inputs: bfloat16 [1024, 8, 1024], P('ctx', 'fsdp'), may hold values from -6 to 6
- cotangent: bfloat16 [1024, 8, 1024], P('ctx', 'fsdp'), may hold values from -6 to 6
- ln1_gain: bfloat16 [1024], P('fsdp'), may hold values from 0.5 to 1.5
- ln1_bias: bfloat16 [1024], P('fsdp'), may hold values from -4 to 4
- qkv_weight: bfloat16 [3, 1024, 1024], P(None, 'fsdp', 'tp'), may hold values from -0.25 to 0.25
- qv_bias: bfloat16 [2, 16, 64], P(None, 'tp', 'fsdp'), may hold values from -6 to 6
- proj_weight: bfloat16 [1024, 1024], P('tp', 'fsdp'), may hold values from -0.375 to 0.375
- proj_bias: bfloat16 [1024], P('fsdp'), may hold values from -4 to 4
- ln2_gain: bfloat16 [1024], P('fsdp'), may hold values from 0.5 to 1.5
- ln2_bias: bfloat16 [1024], P('fsdp'), may hold values from -4 to 4
- fc_weight: bfloat16 [1024, 4096], P('fsdp', 'tp'), may hold values from -0.1875 to 0.1875
- fc_bias: bfloat16 [64, 64], P('tp', 'fsdp'), may hold values from -6 to 6
- fc2_weight: bfloat16 [4096, 1024], P('tp', 'fsdp'), may hold values from -0.09375 to 0.09375
- fc2_bias: bfloat16 [1024], P('fsdp'), may hold values from -4 to 4
Outputs:
- output: bfloat16 [1024, 8, 1024], P(('ctx', 'tp'), 'fsdp')
- input_grad: bfloat16 [1024, 8, 1024], P(('ctx', 'tp'), 'fsdp')
- grad_ln1_gain: float32 [1024], P('fsdp')
- grad_ln1_bias: float32 [1024], P('fsdp')
- grad_qkv_weight: float32 [3, 1024, 1024], P(None, 'fsdp', 'tp')
- grad_qv_bias: float32 [2, 16, 64], P(None, 'tp', 'fsdp')
- grad_proj_weight: float32 [1024, 1024], P('tp', 'fsdp')
- grad_proj_bias: float32 [1024], P('fsdp')
- grad_ln2_gain: float32 [1024], P('fsdp')
- grad_ln2_bias: float32 [1024], P('fsdp')
- grad_fc_weight: float32 [1024, 4096], P('fsdp', 'tp')
- grad_fc_bias: float32 [64, 64], P('tp', 'fsdp')
- grad_fc2_weight: float32 [4096, 1024], P('tp', 'fsdp')
- grad_fc2_bias: float32 [1024], P('fsdp')
All inputs are finite; a program needn't handle non-finite values.
Results may differ from a plain program's by a relative error of at most 0.015.
The roundings to bfloat16 on the way count: a program that leaves them out, or rounds other values in their place, can miss the bound.
Values may be sent and summed in bfloat16 or wider, within the bound.
No kernel may reach another device: no remote copies, remote signals or barrier semaphores. Data moves between devices by JAX's collectives and lax.ppermute only.
A program may use at most 256 MiB of HBM per device.

v0:
```python
from functools import partial
import math

import jax
import jax.numpy as jnp
from jax import lax
from jax.experimental import pallas as pl
from jax.experimental.pallas import tpu as pltpu
from jax.sharding import PartitionSpec as P


HD = 64
BLOCK = 256


EPSILON = 1e-05
NEGATIVE = -1e30
SUB_ROWS = 512


def norm_forward(values, gain, shift):
    centred = values - jnp.mean(values, axis=-1, keepdims=True)
    spread = lax.rsqrt(jnp.mean(centred * centred, axis=-1, keepdims=True) + EPSILON)
    normed = centred * spread
    return (normed * gain + shift, normed, spread)


def norm_backward(grad_out, normed, spread, gain):
    scaled = grad_out * gain
    return spread * (
        scaled
        - jnp.mean(scaled, axis=-1, keepdims=True)
        - normed * jnp.mean(scaled * normed, axis=-1, keepdims=True)
    )


def left_inner(left, right):
    return lax.dot_general(
        left, right, (((0,), (0,)), ((), ())), preferred_element_type=jnp.float32
    )


def right_inner(left, right):
    return lax.dot_general(
        left, right, (((1,), (1,)), ((), ())), preferred_element_type=jnp.float32
    )


def split_heads(values):
    return values.reshape(values.shape[0], values.shape[1], -1, HD)


def block_scores(query_heads, key_heads, query_pos, key_pos):
    scores = jnp.einsum(
        "qshd,kshd->qshk", query_heads, key_heads, preferred_element_type=jnp.float32
    ) * HD ** (-0.5)
    allowed = key_pos[None, :] // BLOCK <= query_pos[:, None] // BLOCK
    return (scores, allowed[:, None, None, :])


def by_blocks(step_fn, carry, pieces):
    count = pieces[0].shape[0]
    sub_width = math.gcd(count, SUB_ROWS)
    split = tuple(
        (entry.reshape((count // sub_width, sub_width) + entry.shape[1:]) for entry in pieces)
    )

    def advance(state, item):
        block_index, parts = item
        return (step_fn(state, parts, block_index * sub_width), None)

    state, _ = lax.scan(advance, carry, (jnp.arange(count // sub_width, dtype=jnp.int32), split))
    return state


def general_device(
    inputs,
    cotangent,
    ln1_gain,
    ln1_bias,
    qkv_weight,
    qv_bias,
    proj_weight,
    proj_bias,
    ln2_gain,
    ln2_bias,
    fc_weight,
    fc_bias,
    fc2_weight,
    fc2_bias,
):
    row_count, seq_count, model_width = inputs.shape
    tokens = row_count * seq_count
    tp_count = lax.axis_size("tp")
    share_rows = row_count // tp_count
    share_tokens = share_rows * seq_count
    share_first = lax.axis_index("tp") * share_tokens

    def own_rows(values):
        return lax.dynamic_slice_in_dim(values, share_first, share_tokens, 0)

    gathered = (
        lax.all_gather(ln1_gain, "fsdp", axis=0, tiled=True),
        lax.all_gather(ln1_bias, "fsdp", axis=0, tiled=True),
        lax.all_gather(qkv_weight, "fsdp", axis=1, tiled=True),
        lax.all_gather(qv_bias, "fsdp", axis=2, tiled=True),
        lax.all_gather(proj_weight, "fsdp", axis=1, tiled=True),
        lax.all_gather(proj_bias, "fsdp", axis=0, tiled=True),
        lax.all_gather(ln2_gain, "fsdp", axis=0, tiled=True),
        lax.all_gather(ln2_bias, "fsdp", axis=0, tiled=True),
        lax.all_gather(fc_weight, "fsdp", axis=0, tiled=True),
        lax.all_gather(fc_bias, "fsdp", axis=1, tiled=True),
        lax.all_gather(fc2_weight, "fsdp", axis=1, tiled=True),
        lax.all_gather(fc2_bias, "fsdp", axis=0, tiled=True),
    )
    (
        gain_one,
        shift_one,
        qkv_full,
        bias_qv,
        proj_full,
        bias_proj,
        gain_two,
        shift_two,
        fc_full,
        bias_fc,
        fc2_full,
        bias_fc2,
    ) = gathered
    head_width = qkv_full.shape[2]
    gain_one_f = gain_one.astype(jnp.float32)
    gain_two_f = gain_two.astype(jnp.float32)
    flat = inputs.reshape(tokens, model_width).astype(jnp.float32)
    first_f, normed_one, spread_one = norm_forward(flat, gain_one_f, shift_one.astype(jnp.float32))
    first_in = first_f.astype(jnp.bfloat16)
    bias_rows = bias_qv.reshape(2, head_width).astype(jnp.float32)
    projected = jnp.einsum("td,cdf->ctf", first_in, qkv_full, preferred_element_type=jnp.float32)
    query_three = (
        (projected[0] + bias_rows[0]).astype(jnp.bfloat16).reshape(row_count, seq_count, head_width)
    )
    key_three = projected[1].astype(jnp.bfloat16).reshape(row_count, seq_count, head_width)
    value_three = (
        (projected[2] + bias_rows[1]).astype(jnp.bfloat16).reshape(row_count, seq_count, head_width)
    )
    query_heads = split_heads(query_three)
    key_heads = split_heads(key_three)
    value_heads = split_heads(value_three)
    local_heads = query_heads.shape[2]
    cycle_place = lax.axis_index("ctx")
    my_first = cycle_place * row_count
    my_pos = my_first + jnp.arange(row_count, dtype=jnp.int32)
    last_block = (my_first + row_count - 1) // BLOCK
    scale = HD ** (-0.5)

    def forward_step(state, parts, first_row):
        key_part, value_part = parts
        key_pos = first_row + jnp.arange(key_part.shape[0], dtype=jnp.int32)

        def update(inner):
            acc_sum, row_top, denom_sum = inner
            scores, allowed = block_scores(query_heads, split_heads(key_part), my_pos, key_pos)
            scores = jnp.where(allowed, scores, NEGATIVE)
            new_top = jnp.maximum(row_top, jnp.max(scores, axis=-1))
            rescale = jnp.exp(row_top - new_top)
            block_weights = jnp.where(allowed, jnp.exp(scores - new_top[..., None]), 0.0)
            denom_sum = denom_sum * rescale + jnp.sum(block_weights, axis=-1)
            acc_sum = acc_sum * rescale[..., None] + jnp.einsum(
                "qshk,kshd->qshd",
                block_weights.astype(jnp.bfloat16),
                split_heads(value_part),
                preferred_element_type=jnp.float32,
            )
            return (acc_sum, new_top, denom_sum)

        return lax.cond(first_row // BLOCK > last_block, lambda inner: inner, update, state)

    stat_shape = (row_count, seq_count, local_heads)
    start_state = (
        jnp.zeros(query_heads.shape, jnp.float32),
        jnp.full(stat_shape, NEGATIVE, jnp.float32),
        jnp.zeros(stat_shape, jnp.float32),
    )
    acc_sum, row_top, denom_sum = by_blocks(
        forward_step,
        start_state,
        (
            lax.all_gather(key_three, "ctx", axis=0, tiled=True),
            lax.all_gather(value_three, "ctx", axis=0, tiled=True),
        ),
    )
    attended_f = acc_sum / denom_sum[..., None]
    log_total = row_top + jnp.log(denom_sum)
    attended = attended_f.reshape(tokens, head_width).astype(jnp.bfloat16)
    attn_term = jnp.dot(attended, proj_full, preferred_element_type=jnp.float32)
    mixed_rows = flat + lax.psum(attn_term, "tp") + bias_proj.astype(jnp.float32)
    second_f, normed_two, spread_two = norm_forward(
        mixed_rows, gain_two_f, shift_two.astype(jnp.float32)
    )
    second_in = second_f.astype(jnp.bfloat16)
    pre_act = jnp.dot(second_in, fc_full, preferred_element_type=jnp.float32) + bias_fc.reshape(
        -1
    ).astype(jnp.float32)
    activated, gelu_pull = jax.vjp(partial(jax.nn.gelu, approximate=True), pre_act)
    hidden = activated.astype(jnp.bfloat16)
    mlp_term = jnp.dot(hidden, fc2_full, preferred_element_type=jnp.float32)
    final_share = own_rows(mixed_rows + lax.psum(mlp_term, "tp") + bias_fc2.astype(jnp.float32))
    output = final_share.astype(jnp.bfloat16).reshape(share_rows, seq_count, model_width)
    grad_rows = cotangent.reshape(tokens, model_width)
    grad_y = grad_rows.astype(jnp.float32)
    grad_bias_fc2 = jnp.sum(grad_y, axis=0)
    grad_fc2 = left_inner(hidden, grad_rows)
    hidden_grad = right_inner(grad_rows, fc2_full)
    (pre_grad_f,) = gelu_pull(hidden_grad)
    pre_grad = pre_grad_f.astype(jnp.bfloat16)
    grad_bias_fc = jnp.sum(pre_grad.astype(jnp.float32), axis=0)
    grad_fc = left_inner(second_in, pre_grad)
    second_term = right_inner(pre_grad, fc_full)
    second_grad = lax.psum(second_term, "tp")
    grad_gain_two = jnp.sum(second_grad * normed_two, axis=0)
    grad_shift_two = jnp.sum(second_grad, axis=0)
    mixed_grad = grad_y + norm_backward(second_grad, normed_two, spread_two, gain_two_f)
    branch_grad = mixed_grad.astype(jnp.bfloat16)
    grad_bias_proj = jnp.sum(branch_grad.astype(jnp.float32), axis=0)
    grad_proj = left_inner(attended, branch_grad)
    attended_grad = right_inner(branch_grad, proj_full).astype(jnp.bfloat16)
    grad_three = attended_grad.reshape(row_count, seq_count, head_width)
    grad_heads = split_heads(grad_three)
    delta_rows = jnp.sum(grad_heads.astype(jnp.float32) * attended_f, axis=-1)
    lse_all, delta_all = (
        lax.all_gather(log_total, "ctx", axis=0, tiled=True),
        lax.all_gather(delta_rows, "ctx", axis=0, tiled=True),
    )

    def back_step(state, parts, first_row):
        query_part_flat, key_part_flat, value_part_flat, grad_part_flat = parts
        count = query_part_flat.shape[0]
        other_pos = first_row + jnp.arange(count, dtype=jnp.int32)
        query_acc, key_acc, value_acc = state

        def query_update(acc_in):
            key_part = split_heads(key_part_flat)
            scores, allowed = block_scores(query_heads, key_part, my_pos, other_pos)
            attn_prob = jnp.where(allowed, jnp.exp(scores - log_total[..., None]), 0.0)
            prob_grad = jnp.einsum(
                "qshd,kshd->qshk",
                grad_heads,
                split_heads(value_part_flat),
                preferred_element_type=jnp.float32,
            )
            score_grad = (attn_prob * (prob_grad - delta_rows[..., None])).astype(jnp.bfloat16)
            return (
                acc_in
                + jnp.einsum(
                    "qshk,kshd->qshd", score_grad, key_part, preferred_element_type=jnp.float32
                )
                * scale
            )

        def key_update(inner):
            key_in, value_in = inner
            lse_part = lax.dynamic_slice_in_dim(lse_all, first_row, count, 0)
            delta_part = lax.dynamic_slice_in_dim(delta_all, first_row, count, 0)
            query_part = split_heads(query_part_flat)
            grad_part = split_heads(grad_part_flat)
            scores, allowed = block_scores(query_part, key_heads, other_pos, my_pos)
            attn_prob = jnp.where(allowed, jnp.exp(scores - lse_part[..., None]), 0.0)
            prob_grad = jnp.einsum(
                "qshd,kshd->qshk", grad_part, value_heads, preferred_element_type=jnp.float32
            )
            score_grad = (attn_prob * (prob_grad - delta_part[..., None])).astype(jnp.bfloat16)
            key_in = (
                key_in
                + jnp.einsum(
                    "qshk,qshd->kshd", score_grad, query_part, preferred_element_type=jnp.float32
                )
                * scale
            )
            value_in = value_in + jnp.einsum(
                "qshk,qshd->kshd",
                attn_prob.astype(jnp.bfloat16),
                grad_part,
                preferred_element_type=jnp.float32,
            )
            return (key_in, value_in)

        query_acc = lax.cond(
            first_row // BLOCK > last_block, lambda acc_in: acc_in, query_update, query_acc
        )
        key_acc, value_acc = lax.cond(
            my_first // BLOCK > (first_row + count - 1) // BLOCK,
            lambda inner: inner,
            key_update,
            (key_acc, value_acc),
        )
        return (query_acc, key_acc, value_acc)

    zero_heads = jnp.zeros(query_heads.shape, jnp.float32)
    query_grad_f, key_grad_f, value_grad_f = by_blocks(
        back_step,
        (zero_heads, zero_heads, zero_heads),
        (
            lax.all_gather(query_three, "ctx", axis=0, tiled=True),
            lax.all_gather(key_three, "ctx", axis=0, tiled=True),
            lax.all_gather(value_three, "ctx", axis=0, tiled=True),
            lax.all_gather(grad_three, "ctx", axis=0, tiled=True),
        ),
    )
    query_grad = query_grad_f.reshape(tokens, head_width).astype(jnp.bfloat16)
    key_grad = key_grad_f.reshape(tokens, head_width).astype(jnp.bfloat16)
    value_grad = value_grad_f.reshape(tokens, head_width).astype(jnp.bfloat16)
    stacked_grad = jnp.stack([query_grad, key_grad, value_grad])
    grad_bias_qv = jnp.stack(
        [
            jnp.sum(query_grad.astype(jnp.float32), axis=0),
            jnp.sum(value_grad.astype(jnp.float32), axis=0),
        ]
    ).reshape(bias_qv.shape)
    grad_qkv = jnp.einsum("td,ctf->cdf", first_in, stacked_grad, preferred_element_type=jnp.float32)
    first_term = jnp.einsum(
        "ctf,cdf->td", stacked_grad, qkv_full, preferred_element_type=jnp.float32
    )
    first_grad = lax.psum(first_term, "tp")
    grad_gain_one = jnp.sum(first_grad * normed_one, axis=0)
    grad_shift_one = jnp.sum(first_grad, axis=0)
    input_rows = own_rows(
        mixed_grad + norm_backward(first_grad, normed_one, spread_one, gain_one_f)
    )
    input_grad = input_rows.astype(jnp.bfloat16).reshape(share_rows, seq_count, model_width)
    shares = (
        lax.psum_scatter(grad_gain_one, ("fsdp", "ctx"), scatter_dimension=0, tiled=True),
        lax.psum_scatter(grad_shift_one, ("fsdp", "ctx"), scatter_dimension=0, tiled=True),
        lax.psum_scatter(grad_qkv, ("fsdp", "ctx"), scatter_dimension=1, tiled=True),
        lax.psum_scatter(grad_bias_qv, ("fsdp", "ctx"), scatter_dimension=2, tiled=True),
        lax.psum_scatter(grad_proj, ("fsdp", "ctx"), scatter_dimension=1, tiled=True),
        lax.psum_scatter(grad_bias_proj, ("fsdp", "ctx"), scatter_dimension=0, tiled=True),
        lax.psum_scatter(grad_gain_two, ("fsdp", "ctx"), scatter_dimension=0, tiled=True),
        lax.psum_scatter(grad_shift_two, ("fsdp", "ctx"), scatter_dimension=0, tiled=True),
        lax.psum_scatter(grad_fc, ("fsdp", "ctx"), scatter_dimension=0, tiled=True),
        lax.psum_scatter(
            grad_bias_fc.reshape(bias_fc.shape), ("fsdp", "ctx"), scatter_dimension=1, tiled=True
        ),
        lax.psum_scatter(grad_fc2, ("fsdp", "ctx"), scatter_dimension=1, tiled=True),
        lax.psum_scatter(grad_bias_fc2, ("fsdp", "ctx"), scatter_dimension=0, tiled=True),
    )
    summed = (
        lax.all_gather(shares[0], "ctx", axis=0, tiled=True),
        lax.all_gather(shares[1], "ctx", axis=0, tiled=True),
        lax.all_gather(shares[2], "ctx", axis=1, tiled=True),
        lax.all_gather(shares[3], "ctx", axis=2, tiled=True),
        lax.all_gather(shares[4], "ctx", axis=1, tiled=True),
        lax.all_gather(shares[5], "ctx", axis=0, tiled=True),
        lax.all_gather(shares[6], "ctx", axis=0, tiled=True),
        lax.all_gather(shares[7], "ctx", axis=0, tiled=True),
        lax.all_gather(shares[8], "ctx", axis=0, tiled=True),
        lax.all_gather(shares[9], "ctx", axis=1, tiled=True),
        lax.all_gather(shares[10], "ctx", axis=1, tiled=True),
        lax.all_gather(shares[11], "ctx", axis=0, tiled=True),
    )
    return (
        output,
        input_grad,
        summed[0],
        summed[1],
        summed[2],
        summed[3],
        summed[4],
        summed[5],
        summed[6],
        summed[7],
        summed[8],
        summed[9],
        summed[10],
        summed[11],
    )


SWAP = ((0, 1), (1, 0))
MATE = ((0, 1), (1, 0), (2, 3), (3, 2))
PEER = ((0, 2), (2, 0), (1, 3), (3, 1))
INWARD = ((0, 1), (3, 2))
MIDDLE = ((1, 2), (2, 1))
OUTWARD = ((1, 0), (2, 3))


def xor_pairs(count, mask):
    return tuple((place, place ^ mask) for place in range(count))


def bf(values):
    return values.astype(jnp.bfloat16)


def f32(values):
    return values.astype(jnp.float32)


def matmul(left, right):
    return jnp.dot(left, right, preferred_element_type=jnp.float32)


def contract(left, right, left_dim, right_dim):
    return lax.dot_general(
        left,
        right,
        (((left_dim,), (right_dim,)), ((), ())),
        preferred_element_type=jnp.float32,
    )


def merged(values):
    return values.reshape(-1, values.shape[-1])


def stack_heads(values):
    heads = values.shape[-1] // HD
    lane_head = lax.broadcasted_iota(jnp.int32, values.shape, 1) // HD
    blank = jnp.zeros_like(values)
    return jnp.concatenate(
        [jnp.where(lane_head == head, values, blank) for head in range(heads)], axis=0
    )


def attend_kernel(query_ref, key_ref, value_ref, out_ref, lse_ref, score_ref, acc_ref):
    block = pl.program_id(0)
    query = merged(query_ref[:, 0])
    rows, width = query.shape
    heads = width // HD
    scale = HD ** (-0.5)

    def score(other, top):
        values = contract(stack_heads(merged(key_ref[:, other])), query, 1, 1)
        values = values.reshape(heads, rows, rows)
        score_ref[other] = values
        return jnp.maximum(top, jnp.max(values, axis=1, keepdims=True))

    top = lax.fori_loop(0, block + 1, score, jnp.full((heads, 1, rows), NEGATIVE, jnp.float32))

    def weigh(other, total):
        values = jnp.exp((score_ref[other] - top) * scale)
        score_ref[other] = values
        return total + jnp.sum(values, axis=1, keepdims=True)

    total = lax.fori_loop(0, block + 1, weigh, jnp.zeros((heads, 1, rows), jnp.float32))
    lse_ref[0] = top * scale + jnp.log(total)
    inverse = 1.0 / total
    acc_ref[...] = jnp.zeros_like(acc_ref)

    def mix(other, unused):
        prob = bf(score_ref[other] * inverse).reshape(heads * rows, rows)
        acc_ref[...] += contract(prob, stack_heads(merged(value_ref[:, other])), 0, 0)
        return unused

    lax.fori_loop(0, block + 1, mix, 0)
    out_ref[:, 0] = bf(acc_ref[...]).reshape(out_ref.shape[0], out_ref.shape[2], width)


def attend_back_kernel(
    query_ref,
    key_ref,
    value_ref,
    out_ref,
    grad_ref,
    lse_ref,
    qkv_grad_ref,
    query_acc,
    key_acc,
    value_acc,
    query_stack,
    grad_stack,
):
    block = pl.program_id(0)
    blocks = pl.num_programs(0)
    query = merged(query_ref[:, 0])
    grad = merged(grad_ref[:, 0])
    rows, width = query.shape
    heads = width // HD
    lane_head = lax.broadcasted_iota(jnp.int32, (rows, width), 1) // HD
    scale = HD ** (-0.5)
    query_stack[...] = stack_heads(query)
    grad_stack[...] = stack_heads(grad)
    products = f32(grad) * f32(merged(out_ref[:, 0]))
    deltas = []
    for head in range(heads):
        column = jnp.sum(jnp.where(lane_head == head, products, 0.0), axis=1, keepdims=True)
        deltas.append(jnp.transpose(jnp.broadcast_to(column, (rows, 128)))[0:1])
    delta = jnp.concatenate(deltas, axis=1)
    lse = jnp.concatenate([lse_ref[0, head] for head in range(heads)], axis=1)
    query_acc[...] = jnp.zeros_like(query_acc)

    @pl.when(block == 0)
    def clear():
        key_acc[...] = jnp.zeros_like(key_acc)
        value_acc[...] = jnp.zeros_like(value_acc)

    def one_block(other, unused):
        key = merged(key_ref[:, other])
        scores = contract(key, query_stack[...], 1, 1)
        prob_grad = contract(merged(value_ref[:, other]), grad_stack[...], 1, 1)
        prob = jnp.exp(scores * scale - lse)
        score_grad = bf(prob * (prob_grad - delta))
        value_acc[other] += contract(bf(prob), grad_stack[...], 1, 0)
        key_acc[other] += contract(score_grad, query_stack[...], 1, 0)
        tall = jnp.concatenate(
            [score_grad[:, head * rows : (head + 1) * rows] for head in range(heads)], axis=0
        )
        query_acc[...] += contract(tall, stack_heads(key), 0, 0)
        return unused

    lax.fori_loop(0, block + 1, one_block, 0)
    slots, _, part, _ = qkv_grad_ref.shape

    def place(which, other, values):
        qkv_grad_ref[:, other, :, which * width : (which + 1) * width] = bf(values).reshape(
            slots, part, width
        )

    place(0, block, query_acc[...] * scale)

    @pl.when(block == blocks - 1)
    def finish():
        for other in range(key_acc.shape[0]):
            place(1, other, key_acc[other] * scale)
            place(2, other, value_acc[other])


def attend_specs(qkv):
    slots, blocks, part, width = qkv.shape
    width //= 3
    one = pl.BlockSpec((slots, 1, part, width), lambda i: (0, i, 0, 0))
    key = pl.BlockSpec((slots, blocks, part, width), lambda i: (0, 0, 0, 1))
    value = pl.BlockSpec((slots, blocks, part, width), lambda i: (0, 0, 0, 2))
    return slots, blocks, part, width, one, key, value


def attend(qkv):
    slots, blocks, part, width, one, key, value = attend_specs(qkv)
    rows = slots * part
    heads = width // HD
    pairs = blocks * (blocks + 1) // 2 * heads
    return pl.pallas_call(
        attend_kernel,
        grid=(blocks,),
        in_specs=[one, key, value],
        out_specs=[one, pl.BlockSpec((1, heads, 1, rows), lambda i: (i, 0, 0, 0))],
        out_shape=[
            jax.ShapeDtypeStruct((slots, blocks, part, width), jnp.bfloat16),
            jax.ShapeDtypeStruct((blocks, heads, 1, rows), jnp.float32),
        ],
        scratch_shapes=[
            pltpu.VMEM((blocks, heads, rows, rows), jnp.float32),
            pltpu.VMEM((rows, width), jnp.float32),
        ],
        cost_estimate=pl.CostEstimate(
            flops=pairs * 4 * rows * rows * width,
            bytes_accessed=8 * qkv.size // 3,
            transcendentals=pairs * rows * rows,
        ),
        name="attend",
    )(qkv, qkv, qkv)


def attend_back(qkv, out, grad, lse):
    slots, blocks, part, width, one, key, value = attend_specs(qkv)
    rows = slots * part
    heads = width // HD
    pairs = blocks * (blocks + 1) // 2 * heads
    return pl.pallas_call(
        attend_back_kernel,
        grid=(blocks,),
        in_specs=[
            one,
            key,
            value,
            one,
            one,
            pl.BlockSpec((1, heads, 1, rows), lambda i: (i, 0, 0, 0)),
        ],
        out_specs=pl.BlockSpec(qkv.shape, lambda i: (0, 0, 0, 0)),
        out_shape=jax.ShapeDtypeStruct(qkv.shape, jnp.bfloat16),
        scratch_shapes=[
            pltpu.VMEM((rows, width), jnp.float32),
            pltpu.VMEM((blocks, rows, width), jnp.float32),
            pltpu.VMEM((blocks, rows, width), jnp.float32),
            pltpu.VMEM((heads * rows, width), jnp.bfloat16),
            pltpu.VMEM((heads * rows, width), jnp.bfloat16),
        ],
        cost_estimate=pl.CostEstimate(
            flops=pairs * 10 * rows * rows * width,
            bytes_accessed=16 * qkv.size // 3,
            transcendentals=pairs * rows * rows,
        ),
        name="attend_back",
    )(qkv, qkv, qkv, out, grad, lse)


def unit_mask(rows, width, start):
    row = lax.broadcasted_iota(jnp.int32, (rows, width), 0)
    unit = lax.broadcasted_iota(jnp.int32, (rows, width), 1) - start
    return jnp.logical_and(unit >= 0, unit // HD == row)


def pick_matrix(width, shift):
    column = lax.broadcasted_iota(jnp.int32, (HD // 2, width), 0)
    unit = lax.broadcasted_iota(jnp.int32, (HD // 2, width), 1)
    return f32(unit % HD == column + shift)


def pack_params_kernel(*refs):
    vectors, qv_ref, fc_ref, out_ref, scratch = refs[:6], *refs[6:]
    scratch[...] = jnp.zeros_like(scratch)
    for row, vector in enumerate(vectors):
        scratch[row, :] = f32(vector[...])
    heads = qv_ref.shape[1]
    part = qv_ref.shape[2]
    for which in range(2):
        scratch[8 + which * heads : 8 + (which + 1) * heads, :part] = f32(qv_ref[which])
        scratch[8:16, 128 * (which + 1) : 128 * (which + 1) + part] = f32(
            fc_ref[8 * which : 8 * which + 8, :]
        )
    out_ref[...] = bf(scratch[...])


def pack_params(vectors, qv_bias, fc_bias):
    shape = (16, vectors[0].shape[0])
    return pl.pallas_call(
        pack_params_kernel,
        out_shape=jax.ShapeDtypeStruct(shape, jnp.bfloat16),
        scratch_shapes=[pltpu.VMEM(shape, jnp.float32)],
        name="pack_params",
    )(*vectors, qv_bias, fc_bias)


def low_high(flag, own, other):
    return jnp.where(flag == 0, own, other), jnp.where(flag == 0, other, own)


def unpack_params_kernel(flag_ref, own_ref, other_ref, vector_ref, qkv_ref, fc_ref):
    flag = flag_ref[0]
    own = f32(own_ref[...])
    other = f32(other_ref[...])
    vector_ref[...] = jnp.concatenate([own[:8], other[:8]], axis=1)
    part = HD // 2

    def spread(width, column):
        low, high = low_high(
            flag, own[8:16, column : column + part], other[8:16, column : column + part]
        )
        return matmul(low, pick_matrix(width, 0)) + matmul(high, pick_matrix(width, part))

    def row_of(values, mask):
        return jnp.sum(jnp.where(mask, values, 0.0), axis=0, keepdims=True)

    width = qkv_ref.shape[1]
    third = width // 3
    heads = third // HD
    row = lax.broadcasted_iota(jnp.int32, (8, width), 0)
    query_mask = jnp.logical_and(unit_mask(8, width, 0), row < heads)
    value_mask = unit_mask(8, width, 2 * third - heads * HD)
    value_mask = jnp.logical_and(value_mask, row >= heads)
    qkv_ref[...] = row_of(spread(width, 0), jnp.logical_or(query_mask, value_mask))
    width = fc_ref.shape[1]
    fc_ref[...] = row_of(spread(width, 128), unit_mask(8, width, 0)) + row_of(
        spread(width, 256), unit_mask(8, width, 8 * HD)
    )


def unpack_params(flag, own, other, qkv_width, fc_width):
    whole = pl.BlockSpec(memory_space=pltpu.VMEM)
    return pl.pallas_call(
        unpack_params_kernel,
        in_specs=[pl.BlockSpec(memory_space=pltpu.SMEM), whole, whole],
        out_shape=[
            jax.ShapeDtypeStruct((8, 2 * own.shape[1]), jnp.float32),
            jax.ShapeDtypeStruct((1, qkv_width), jnp.float32),
            jax.ShapeDtypeStruct((1, fc_width), jnp.float32),
        ],
        name="unpack_params",
    )(flag, own, other)


def pack_sums_kernel(flag_ref, *refs):
    vectors, qkv_ref, fc_ref, kept_ref, sent_ref = refs[:6], *refs[6:]
    flag = flag_ref[0]
    half = kept_ref.shape[1]
    part = HD // 2
    kept_ref[...] = jnp.zeros_like(kept_ref)
    sent_ref[...] = jnp.zeros_like(sent_ref)
    for row, vector in enumerate(vectors):
        kept_ref[row, :] = vector[:half]
        sent_ref[row, :] = vector[half:]

    def take(mask, values, column):
        spread = jnp.where(mask, jnp.broadcast_to(values, mask.shape), 0.0)

        def pick(shift):
            return lax.dot_general(
                spread,
                pick_matrix(mask.shape[1], shift),
                (((1,), (1,)), ((), ())),
                precision=lax.Precision.HIGHEST,
                preferred_element_type=jnp.float32,
            )

        kept, sent = low_high(flag, pick(0), pick(part))
        kept_ref[8:16, column : column + part] = kept
        sent_ref[8:16, column : column + part] = sent

    width = qkv_ref.shape[0]
    third = width // 3
    heads = third // HD
    row = lax.broadcasted_iota(jnp.int32, (8, width), 0)
    query_mask = jnp.logical_and(unit_mask(8, width, 0), row < heads)
    value_mask = jnp.logical_and(unit_mask(8, width, 2 * third - heads * HD), row >= heads)
    take(jnp.logical_or(query_mask, value_mask), qkv_ref[...].reshape(1, width), 0)
    width = fc_ref.shape[0]
    values = fc_ref[...].reshape(1, width)
    take(unit_mask(8, width, 0), values, 128)
    take(unit_mask(8, width, 8 * HD), values, 256)


def pack_sums(flag, vectors, sum_qkv, sum_fc):
    whole = pl.BlockSpec(memory_space=pltpu.VMEM)
    shape = jax.ShapeDtypeStruct((16, vectors[0].shape[0] // 2), jnp.float32)
    return pl.pallas_call(
        pack_sums_kernel,
        in_specs=[pl.BlockSpec(memory_space=pltpu.SMEM)] + [whole] * 8,
        out_shape=[shape, shape],
        name="pack_sums",
    )(flag, *vectors, sum_qkv, sum_fc)


def unpack_sums_kernel(sums_ref, *refs):
    vectors, qv_ref, fc_ref = refs[:6], *refs[6:]
    for row, vector in enumerate(vectors):
        vector[...] = sums_ref[row, :]
    heads, part = qv_ref.shape[1:]
    for which in range(2):
        qv_ref[which] = sums_ref[8 + which * heads : 8 + (which + 1) * heads, :part]
        fc_ref[8 * which : 8 * which + 8, :] = sums_ref[
            8:16, 128 * (which + 1) : 128 * (which + 1) + part
        ]


def unpack_sums(sums, qv_shape, fc_shape):
    vector = jax.ShapeDtypeStruct((sums.shape[1],), jnp.float32)
    return pl.pallas_call(
        unpack_sums_kernel,
        out_shape=[vector] * 6
        + [jax.ShapeDtypeStruct(qv_shape, jnp.float32), jax.ShapeDtypeStruct(fc_shape, jnp.float32)],
        name="unpack_sums",
    )(sums)


def spread_parts(values):
    mate = lax.ppermute(values, "tp", MATE)
    peer = lax.ppermute(values, "tp", PEER)
    across = lax.ppermute(peer, "tp", MATE)
    return (values, mate, peer, across)


def gather_sum(part_of):
    across = lax.ppermute(bf(part_of(3)), "tp", MATE)
    peer = lax.ppermute(bf(part_of(2) + f32(across)), "tp", PEER)
    mate = lax.ppermute(bf(part_of(1)), "tp", MATE)
    return part_of(0) + f32(mate) + f32(peer)


def join_rows(parts):
    return lax.optimization_barrier(jnp.concatenate(parts, axis=0))


def sum_halves(half_of):
    sent = bf(half_of(1))
    other = lax.ppermute(sent, "fsdp", SWAP)
    return bf(half_of(0) + f32(other))


def sum_chained(half_of):
    half = sum_halves(half_of)
    edge = lax.ppermute(half, "ctx", INWARD)
    pair = bf(f32(half) + f32(edge))
    middle = lax.ppermute(pair, "ctx", MIDDLE)
    total = bf(f32(pair) + f32(middle))
    outer = lax.ppermute(total, "ctx", OUTWARD)
    place = lax.axis_index("ctx")
    inner = jnp.logical_and(place > 0, place < 3)
    return f32(jnp.where(inner, total, outer))


def fast_device(
    inputs,
    cotangent,
    ln1_gain,
    ln1_bias,
    qkv_weight,
    qv_bias,
    proj_weight,
    proj_bias,
    ln2_gain,
    ln2_bias,
    fc_weight,
    fc_bias,
    fc2_weight,
    fc2_bias,
):
    row_count, _, width = inputs.shape
    tp_count = lax.axis_size("tp")
    ctx_count = lax.axis_size("ctx")
    share_rows = row_count // tp_count
    share_tokens = share_rows * ctx_count
    place_f = lax.axis_index("fsdp")
    place_c = lax.axis_index("ctx")
    place_t = lax.axis_index("tp")
    half = width // 2
    lower = place_f == 0

    def own_first(values):
        flipped = jnp.concatenate([values[..., half:], values[..., :half]], axis=-1)
        return jnp.where(lower, values, flipped)

    def to_sequences(values):
        mine = lax.dynamic_slice_in_dim(values, place_t * share_rows, share_rows, 0)
        mine = own_first(mine)
        got = []
        for step in range(ctx_count):
            piece = lax.dynamic_index_in_dim(mine, place_c ^ step, 1, keepdims=False)
            if step:
                piece = lax.ppermute(piece, "ctx", xor_pairs(ctx_count, step))
            got.append(piece)
        stacked = jnp.stack(got)
        ordered = [
            lax.dynamic_index_in_dim(stacked, place_c ^ step, 0, keepdims=False)
            for step in range(ctx_count)
        ]
        return jnp.concatenate(ordered, axis=0)

    def to_positions(values):
        mine = own_first(values).reshape(ctx_count, share_rows, width)
        got = []
        for step in range(ctx_count):
            piece = lax.dynamic_index_in_dim(mine, place_c ^ step, 0, keepdims=False)
            if step:
                piece = lax.ppermute(piece, "ctx", xor_pairs(ctx_count, step))
            got.append(piece)
        stacked = jnp.stack(got)
        ordered = [
            lax.dynamic_index_in_dim(stacked, place_c ^ step, 0, keepdims=False)
            for step in range(ctx_count)
        ]
        return jnp.stack(ordered, axis=1)

    flat = f32(to_sequences(inputs))

    flag = place_f.astype(jnp.int32).reshape(1)
    small_own = pack_params(
        (ln1_gain, ln1_bias, proj_bias, ln2_gain, ln2_bias, fc2_bias), qv_bias, fc_bias
    )
    small_other = lax.ppermute(small_own, "fsdp", SWAP)
    qkv_other = lax.ppermute(qkv_weight, "fsdp", SWAP)
    proj_other = lax.ppermute(proj_weight, "fsdp", SWAP)
    fc_other = lax.ppermute(fc_weight, "fsdp", SWAP)
    fc2_other = lax.ppermute(fc2_weight, "fsdp", SWAP)
    proj_full = jnp.concatenate([proj_weight, proj_other], axis=1)
    fc_full = jnp.concatenate([fc_weight, fc_other], axis=0)
    fc2_full = jnp.concatenate([fc2_weight, fc2_other], axis=1)
    qkv_full = jnp.concatenate(
        [
            jnp.concatenate([entry[index] for index in range(3)], axis=1)
            for entry in (qkv_weight, qkv_other)
        ],
        axis=0,
    )

    head_width = qkv_weight.shape[2]
    vectors, bias_qkv, bias_row = unpack_params(
        flag, small_own, small_other, 3 * head_width, fc_weight.shape[1]
    )
    gain_one, shift_one, bias_proj, gain_two, shift_two, bias_fc2 = (vectors[n] for n in range(6))

    first_f, normed_one, spread_one = norm_forward(flat, gain_one, shift_one)
    first_in = join_rows(spread_parts(bf(first_f)))
    head_shape = (tp_count, ctx_count, share_rows, head_width)
    qkv = bf(matmul(first_in, qkv_full) + bias_qkv)
    qkv = qkv.reshape(head_shape[:3] + (3 * head_width,))
    attended_four, lse = attend(qkv)
    attended = attended_four.reshape(-1, head_width)

    def rows_of(values, slot):
        return values[slot * share_tokens : (slot + 1) * share_tokens]

    attn_sum = gather_sum(lambda slot: matmul(rows_of(attended, slot), proj_full))
    mixed = flat + attn_sum + bias_proj
    second_f, normed_two, spread_two = norm_forward(mixed, gain_two, shift_two)
    second_in = spread_parts(bf(second_f))

    grad_own = to_sequences(cotangent)
    grad_rows = spread_parts(grad_own)
    grad_y = f32(grad_own)

    hidden = []
    pre_grad = []
    for slot in range(tp_count):
        hidden_grad = contract(grad_rows[slot], fc2_full, 1, 1)
        pre_act = matmul(second_in[slot], fc_full) + bias_row
        activated, gelu_pull = jax.vjp(partial(jax.nn.gelu, approximate=True), pre_act)
        hidden.append(bf(activated))
        pre_grad.append(bf(gelu_pull(hidden_grad)[0]))

    second_grad = gather_sum(lambda slot: contract(pre_grad[slot], fc_full, 1, 1))
    mixed_grad = grad_y + norm_backward(second_grad, normed_two, spread_two, gain_two)
    branch_own = bf(mixed_grad)
    branch = spread_parts(branch_own)

    mlp_sum = gather_sum(lambda slot: matmul(hidden[slot], fc2_full))
    output = to_positions(bf(mixed + mlp_sum + bias_fc2))

    def halved(values, which):
        return values[:, which * half : (which + 1) * half]

    hidden_all = join_rows(hidden)
    pre_grad_all = join_rows(pre_grad)
    second_all = join_rows(second_in)
    grad_all = join_rows(grad_rows)
    grad_fc2 = sum_chained(lambda which: contract(hidden_all, halved(grad_all, which), 0, 0))
    grad_fc = sum_chained(lambda which: contract(halved(second_all, which), pre_grad_all, 0, 0))

    branch = join_rows(branch)
    attended_grad = bf(contract(branch, proj_full, 1, 1)).reshape(head_shape)
    qkv_grad = attend_back(qkv, attended_four, attended_grad, lse).reshape(-1, 3 * head_width)
    grad_proj = sum_chained(lambda which: contract(attended, halved(branch, which), 0, 0))
    grad_qkv = sum_chained(lambda which: contract(halved(first_in, which), qkv_grad, 0, 0))
    grad_qkv = jnp.stack(
        [grad_qkv[:, index * head_width : (index + 1) * head_width] for index in range(3)]
    )

    first_grad = gather_sum(lambda slot: contract(rows_of(qkv_grad, slot), qkv_full, 1, 1))
    input_own = mixed_grad + norm_backward(first_grad, normed_one, spread_one, gain_one)
    input_grad = to_positions(bf(input_own))

    token_sums = (
        jnp.sum(first_grad * normed_one, axis=0),
        jnp.sum(first_grad, axis=0),
        jnp.sum(f32(branch_own), axis=0),
        jnp.sum(second_grad * normed_two, axis=0),
        jnp.sum(second_grad, axis=0),
        jnp.sum(grad_y, axis=0),
    )
    sum_qkv = jnp.sum(f32(qkv_grad), axis=0)
    sum_fc = sum(jnp.sum(f32(part), axis=0) for part in pre_grad)
    kept, sent = pack_sums(flag, token_sums, sum_qkv, sum_fc)
    small = kept + lax.ppermute(sent, "fsdp", SWAP)
    shared = small[:8]
    shared = shared + lax.ppermute(shared, "tp", MATE)
    shared = shared + lax.ppermute(shared, "tp", PEER)
    small = jnp.concatenate([shared, small[8:]], axis=0)
    small = small + lax.ppermute(small, "ctx", xor_pairs(ctx_count, 1))
    small = small + lax.ppermute(small, "ctx", xor_pairs(ctx_count, 2))
    sums = unpack_sums(small, qv_bias.shape, fc_bias.shape)
    return (
        output,
        input_grad,
        sums[0],
        sums[1],
        grad_qkv,
        sums[6],
        grad_proj,
        sums[2],
        sums[3],
        sums[4],
        grad_fc,
        sums[7],
        grad_fc2,
        sums[5],
    )


def on_device(*args):
    rows, sequences, _ = args[0].shape
    whole_sequences = (
        lax.axis_size("fsdp") == 2
        and lax.axis_size("tp") == 4
        and lax.axis_size("ctx") == 4
        and sequences == 4
        and rows == BLOCK
    )
    if not whole_sequences:
        return general_device(*args)
    return fast_device(*args)


def solution(mesh):
    return jax.shard_map(
        on_device,
        mesh=mesh,
        in_specs=(
            P("ctx", "fsdp", None),
            P("ctx", "fsdp", None),
            P("fsdp"),
            P("fsdp"),
            P(None, "fsdp", "tp"),
            P(None, "tp", "fsdp"),
            P("tp", "fsdp"),
            P("fsdp"),
            P("fsdp"),
            P("fsdp"),
            P("fsdp", "tp"),
            P("tp", "fsdp"),
            P("tp", "fsdp"),
            P("fsdp"),
        ),
        out_specs=(
            P(("ctx", "tp"), "fsdp", None),
            P(("ctx", "tp"), "fsdp", None),
            P("fsdp"),
            P("fsdp"),
            P(None, "fsdp", "tp"),
            P(None, "tp", "fsdp"),
            P("tp", "fsdp"),
            P("fsdp"),
            P("fsdp"),
            P("fsdp"),
            P("fsdp", "tp"),
            P("tp", "fsdp"),
            P("tp", "fsdp"),
            P("fsdp"),
        ),
        check_vma=False,
    )
```

profile of v0, /device:TPU:0, one launch (start us, length us, event | category | flops | bytes accessed | tf_op | source)
XLA Modules:
  0.0 408.2 jit_solution(10285653097414080581)
XLA Ops:
  2.1 3.0 collective-permute-start.3
  7.9 4.1 %collective-permute-start.25 = (bf16[64,1024]{1,0:T(8,128)(2,1)}, bf16[64,1024]{1,0:T(8,128)(2,1)S(1)}, u32[]{:S(2)}, u32[]{:S(2)}) collective-permute-start(bf16[64,1024]{1,0:T(8,128)(2,1)} %get-tuple-element.116), channel_id=1, source_target_pairs={{0,12},{4,8},{8,4},{12,0},{1,13},{5,9},{9,5},{13,1},{2,14},{6,10},... | collective-permute-start | bytes 393224 | tf_op jit(solution)/shard_map/ppermute | solution.py:828
  21.0 3.6 collective-permute-start.2
  31.0 3.4 collective-permute-done.1
  37.6 14.7 %collective-permute-done.8 = bf16[256,512]{1,0:T(8,128)(2,1)S(1)} collective-permute-done((bf16[256,512]{1,0:T(8,128)(2,1)S(1)}, bf16[256,512]{1,0:T(8,128)(2,1)S(1)}, u32[]{:S(2)}, u32[]{:S(2)}) %collective-permute-start.8) | collective-permute-done | bytes 262176 | tf_op jit(solution)/shard_map/ppermute | solution.py:860
  54.1 2.3 constant_dynamic-update-slice_fusion.3
  72.2 2.9 add_convert_fusion
  75.2 11.5 %attend.1 = (bf16[4,4,64,256]{3,2,1,0:T(8,128)(2,1)}, f32[4,4,1,256]{3,2,1,0:T(1,128)}) custom-call(bf16[4,4,64,768]{3,2,1,0:T(8,128)(2,1)} %bitcast.213, bf16[4,4,64,768]{3,2,1,0:T(8,128)(2,1)} %bitcast.214, bf16[4,4,64,768]{3,2,1,0:T(8,128)(2,1)} %bitcast.215), custom_call_target="tpu_custom_call" | custom-call | flops 2684354560 | bytes 2097152 | tf_op jit(solution)/shard_map/attend/pallas_call | solution.py:540
  98.0 7.1 %collective-permute-done.11 = bf16[256,1024]{1,0:T(8,128)(2,1)S(1)} collective-permute-done((bf16[256,1024]{1,0:T(8,128)(2,1)S(1)}, bf16[256,1024]{1,0:T(8,128)(2,1)S(1)}, u32[]{:S(2)}, u32[]{:S(2)}) %collective-permute-start.11) | collective-permute-done | bytes 524320 | tf_op jit(solution)/shard_map/ppermute | solution.py:763
  113.4 8.4 %collective-permute-done.16 = bf16[256,1024]{1,0:T(8,128)(2,1)S(1)} collective-permute-done((bf16[256,1024]{1,0:T(8,128)(2,1)S(1)}, bf16[256,1024]{1,0:T(8,128)(2,1)S(1)}, u32[]{:S(2)}, u32[]{:S(2)}) %collective-permute-start.16) | collective-permute-done | bytes 524320 | tf_op jit(solution)/shard_map/ppermute | solution.py:756
  137.8 10.3 %collective-permute-done.31 = bf16[256,1024]{1,0:T(8,128)(2,1)S(1)} collective-permute-done((bf16[256,1024]{1,0:T(8,128)(2,1)S(1)}, bf16[256,1024]{1,0:T(8,128)(2,1)S(1)}, u32[]{:S(2)}, u32[]{:S(2)}) %collective-permute-start.31) | collective-permute-done | bytes 524320 | tf_op jit(solution)/shard_map/ppermute | solution.py:763
  153.4 5.9 %collective-permute-done.19 = bf16[256,1024]{1,0:T(8,128)(2,1)S(1)} collective-permute-done((bf16[256,1024]{1,0:T(8,128)(2,1)S(1)}, bf16[256,1024]{1,0:T(8,128)(2,1)S(1)}, u32[]{:S(2)}, u32[]{:S(2)}) %collective-permute-start.19) | collective-permute-done | bytes 524320 | tf_op jit(solution)/shard_map/ppermute | solution.py:763
  160.4 3.6 collective-permute-start.22
  164.1 13.5 %collective-permute-done.58 = bf16[1024,512]{1,0:T(8,128)(2,1)S(1)} collective-permute-done((bf16[1024,512]{1,0:T(8,128)(2,1)S(1)}, bf16[1024,512]{1,0:T(8,128)(2,1)S(1)}, u32[]{:S(2)}, u32[]{:S(2)}) %collective-permute-start.58) | collective-permute-done | bytes 1048608 | tf_op jit(solution)/shard_map/ppermute | solution.py:774
  177.6 2.8 collective-permute-start.21
  180.4 2.3 add_convert_fusion.3
  184.3 2.4 add_convert_fusion.6
  186.7 3.4 collective-permute-start.55
  190.0 2.2 collective-permute-start.59
  195.4 13.7 %attend_back.1 = bf16[4,4,64,768]{3,2,1,0:T(8,128)(2,1)} custom-call(bf16[4,4,64,768]{3,2,1,0:T(8,128)(2,1)} %bitcast.216, bf16[4,4,64,768]{3,2,1,0:T(8,128)(2,1)} %bitcast.217, bf16[4,4,64,768]{3,2,1,0:T(8,128)(2,1)} %bitcast.218, bf16[4,4,64,256]{3,2,1,0:T(8,128)(2,1)} %get-tuple-element.31.out_ref, bf16[4,4,64,256]{3,2,1,0:T(8,128)(2,1)} %bitcast.219, ...), custom_call_target="tpu_custom_call" | custom-call | flops 6710886400 | bytes 4194304 | tf_op jit(solution)/shard_map/attend_back/pallas_call | solution.py:567
  218.3 2.9 add_convert_fusion.5
  221.2 13.6 %collective-permute-done.59 = bf16[1024,512]{1,0:T(8,128)(2,1)} collective-permute-done((bf16[1024,512]{1,0:T(8,128)(2,1)}, bf16[1024,512]{1,0:T(8,128)(2,1)}, u32[]{:S(2)}, u32[]{:S(2)}) %collective-permute-start.59) | collective-permute-done | bytes 1048608 | tf_op jit(solution)/shard_map/ppermute | solution.py:780
  241.7 5.8 %collective-permute-start.51 = (bf16[256,512]{1,0:T(8,128)(2,1)S(1)}, bf16[256,512]{1,0:T(8,128)(2,1)S(1)}, u32[]{:S(2)}, u32[]{:S(2)}) collective-permute-start(bf16[256,512]{1,0:T(8,128)(2,1)S(1)} %fusion.16), channel_id=1, source_target_pairs={{0,4},{12,8},{1,5},{13,9},{2,6},{14,10},{3,7},{15,11},{16,20},{28,... | collective-permute-start | bytes 786440 | tf_op jit(solution)/shard_map/ppermute | solution.py:780
  248.1 4.2 %collective-permute-done.51 = bf16[256,512]{1,0:T(8,128)(2,1)S(1)} collective-permute-done((bf16[256,512]{1,0:T(8,128)(2,1)S(1)}, bf16[256,512]{1,0:T(8,128)(2,1)S(1)}, u32[]{:S(2)}, u32[]{:S(2)}) %collective-permute-start.51) | collective-permute-done | bytes 262176 | tf_op jit(solution)/shard_map/ppermute | solution.py:780
  255.8 39.2 %collective-permute-start.47 = (bf16[512,768]{1,0:T(8,128)(2,1)S(1)}, bf16[512,768]{1,0:T(8,128)(2,1)}, u32[]{:S(2)}, u32[]{:S(2)}) collective-permute-start(bf16[512,768]{1,0:T(8,128)(2,1)S(1)} %add_convert_fusion.9), channel_id=1, source_target_pairs={{0,4},{12,8},{1,5},{13,9},{2,6},{14,10},{3,7},{15,11},{16,20},{28,... | collective-permute-start | bytes 2359304 | tf_op jit(solution)/shard_map/ppermute | solution.py:780
  313.1 3.7 collective-permute-start.44
  316.8 2.2 add_convert_fusion.8
  319.0 19.9 %collective-permute-done.44 = f32[16,512]{1,0:T(8,128)S(1)} collective-permute-done((f32[16,512]{1,0:T(8,128)S(1)}, f32[16,512]{1,0:T(8,128)S(1)}, u32[]{:S(2)}, u32[]{:S(2)}) %collective-permute-start.44) | collective-permute-done | bytes 32800 | tf_op jit(solution)/shard_map/ppermute | solution.py:956
  345.0 18.7 %collective-permute-done.45 = f32[16,512]{1,0:T(8,128)S(1)} collective-permute-done((f32[16,512]{1,0:T(8,128)S(1)}, f32[16,512]{1,0:T(8,128)S(1)}, u32[]{:S(2)}, u32[]{:S(2)}) %collective-permute-start.45) | collective-permute-done | bytes 32800 | tf_op jit(solution)/shard_map/ppermute | solution.py:957
  375.5 2.7 select_convert_fusion.1
  378.1 14.4 %collective-permute-done.61 = bf16[1024,512]{1,0:T(8,128)(2,1)S(1)} collective-permute-done((bf16[1024,512]{1,0:T(8,128)(2,1)S(1)}, bf16[1024,512]{1,0:T(8,128)(2,1)S(1)}, u32[]{:S(2)}, u32[]{:S(2)}) %collective-permute-start.61) | collective-permute-done | bytes 1048608 | tf_op jit(solution)/shard_map/ppermute | solution.py:784
  394.0 12.5 %collective-permute-done.49 = bf16[512,768]{1,0:T(8,128)(2,1)S(1)} collective-permute-done((bf16[512,768]{1,0:T(8,128)(2,1)S(1)}, bf16[512,768]{1,0:T(8,128)(2,1)S(1)}, u32[]{:S(2)}, u32[]{:S(2)}) %collective-permute-start.49) | collective-permute-done | bytes 786464 | tf_op jit(solution)/shard_map/ppermute | solution.py:784
  (285 shorter events, 145.3 us)
Async XLA Ops:
  5.0 60.2 %collective-permute-start.7 = (bf16[3,512,256]{2,1,0:T(8,128)(2,1)}, bf16[3,512,256]{2,1,0:T(8,128)(2,1)}, u32[]{:S(2)}, u32[]{:S(2)}) collective-permute-start(bf16[3,512,256]{2,1,0:T(8,128)(2,1)} %param.18), channel_id=1, source_target_pairs={{0,16},{16,0},{1,17},{17,1},{2,18},{18,2},{3,19},{19,3},{4,20},{20... | collective-permute-start | bytes 2359304 | tf_op jit(solution)/shard_map/ppermute | solution.py:859
  12.0 55.1 %collective-permute-start.13 = (bf16[1024,512]{1,0:T(8,128)(2,1)}, bf16[1024,512]{1,0:T(8,128)(2,1)}, u32[]{:S(2)}, u32[]{:S(2)}) collective-permute-start(bf16[1024,512]{1,0:T(8,128)(2,1)} %param.26), channel_id=1, source_target_pairs={{0,16},{16,0},{1,17},{17,1},{2,18},{18,2},{3,19},{19,3},{4,20},{20... | collective-permute-start | bytes 3145736 | tf_op jit(solution)/shard_map/ppermute | solution.py:862
  29.4 22.9 %collective-permute-start.8 = (bf16[256,512]{1,0:T(8,128)(2,1)S(1)}, bf16[256,512]{1,0:T(8,128)(2,1)S(1)}, u32[]{:S(2)}, u32[]{:S(2)}) collective-permute-start(bf16[256,512]{1,0:T(8,128)(2,1)S(1)} %copy-done.18), channel_id=1, source_target_pairs={{0,16},{16,0},{1,17},{17,1},{2,18},{18,2},{3,19},{19,3},{4,20},{20... | collective-permute-start | bytes 786440 | tf_op jit(solution)/shard_map/ppermute | solution.py:860
  34.4 26.8 %collective-permute-start.28 = (bf16[256,1024]{1,0:T(8,128)(2,1)S(1)}, bf16[256,1024]{1,0:T(8,128)(2,1)}, u32[]{:S(2)}, u32[]{:S(2)}) collective-permute-start(bf16[256,1024]{1,0:T(8,128)(2,1)S(1)} %get-tuple-element.83), channel_id=1, source_target_pairs={{0,2},{2,0},{1,3},{3,1},{4,6},{6,4},{5,7},{7,5},{8,10},{10,8},{9,1... | collective-permute-start | bytes 1572872 | tf_op jit(solution)/shard_map/ppermute | solution.py:756
  36.0 22.7 %collective-permute-start.26 = (bf16[256,1024]{1,0:T(8,128)(2,1)S(1)}, bf16[256,1024]{1,0:T(8,128)(2,1)}, u32[]{:S(2)}, u32[]{:S(2)}) collective-permute-start(bf16[256,1024]{1,0:T(8,128)(2,1)S(1)} %get-tuple-element.83), channel_id=1, source_target_pairs={{0,1},{1,0},{2,3},{3,2},{4,5},{5,4},{6,7},{7,6},{8,9},{9,8},{10,11... | collective-permute-start | bytes 1572872 | tf_op jit(solution)/shard_map/ppermute | solution.py:755
  58.7 36.1 %collective-permute-start.12 = (bf16[512,1024]{1,0:T(8,128)(2,1)}, bf16[512,1024]{1,0:T(8,128)(2,1)}, u32[]{:S(2)}, u32[]{:S(2)}) collective-permute-start(bf16[512,1024]{1,0:T(8,128)(2,1)} %param.24), channel_id=1, source_target_pairs={{0,16},{16,0},{1,17},{17,1},{2,18},{18,2},{3,19},{19,3},{4,20},{20... | collective-permute-start | bytes 3145736 | tf_op jit(solution)/shard_map/ppermute | solution.py:861
  65.3 30.9 %collective-permute-start.29 = (bf16[256,1024]{1,0:T(8,128)(2,1)}, bf16[256,1024]{1,0:T(8,128)(2,1)}, u32[]{:S(2)}, u32[]{:S(2)}) collective-permute-start(bf16[256,1024]{1,0:T(8,128)(2,1)} %collective-permute-done.28), channel_id=1, source_target_pairs={{0,1},{1,0},{2,3},{3,2},{4,5},{5,4},{6,7},{7,6},{8,9},{9,8},{10,11... | collective-permute-start | bytes 1572872 | tf_op jit(solution)/shard_map/ppermute | solution.py:757
  113.3 40.1 %collective-permute-start.15 = (bf16[256,1024]{1,0:T(8,128)(2,1)S(1)}, bf16[256,1024]{1,0:T(8,128)(2,1)S(1)}, u32[]{:S(2)}, u32[]{:S(2)}) collective-permute-start(bf16[256,1024]{1,0:T(8,128)(2,1)S(1)} %convolution_convert_fusion.9), channel_id=1, source_target_pairs={{0,1},{1,0},{2,3},{3,2},{4,5},{5,4},{6,7},{7,6},{8,9},{9,8},{10,11... | collective-permute-start | bytes 1572872 | tf_op jit(solution)/shard_map/ppermute | solution.py:764
  130.0 52.7 %collective-permute-start.54 = (bf16[512,1024]{1,0:T(8,128)(2,1)S(1)}, bf16[512,1024]{1,0:T(8,128)(2,1)S(1)}, u32[]{:S(2)}, u32[]{:S(2)}) collective-permute-start(bf16[512,1024]{1,0:T(8,128)(2,1)S(1)} %convolution_convert_fusion.1), channel_id=1, source_target_pairs={{0,16},{16,0},{1,17},{17,1},{2,18},{18,2},{3,19},{19,3},{4,20},{20... | collective-permute-start | bytes 3145736 | tf_op jit(solution)/shard_map/ppermute | solution.py:774
  135.4 42.2 %collective-permute-start.58 = (bf16[1024,512]{1,0:T(8,128)(2,1)S(1)}, bf16[1024,512]{1,0:T(8,128)(2,1)S(1)}, u32[]{:S(2)}, u32[]{:S(2)}) collective-permute-start(bf16[1024,512]{1,0:T(8,128)(2,1)S(1)} %convolution_convert_fusion), channel_id=1, source_target_pairs={{0,16},{16,0},{1,17},{17,1},{2,18},{18,2},{3,19},{19,3},{4,20},{20... | collective-permute-start | bytes 3145736 | tf_op jit(solution)/shard_map/ppermute | solution.py:774
  151.9 32.4 %collective-permute-start.33 = (bf16[256,1024]{1,0:T(8,128)(2,1)S(1)}, bf16[256,1024]{1,0:T(8,128)(2,1)S(1)}, u32[]{:S(2)}, u32[]{:S(2)}) collective-permute-start(bf16[256,1024]{1,0:T(8,128)(2,1)S(1)} %get-tuple-element.85), channel_id=1, source_target_pairs={{0,2},{2,0},{1,3},{3,1},{4,6},{6,4},{5,7},{7,5},{8,10},{10,8},{9,1... | collective-permute-start | bytes 1572872 | tf_op jit(solution)/shard_map/ppermute | solution.py:756
  153.4 40.3 %collective-permute-start.32 = (bf16[256,1024]{1,0:T(8,128)(2,1)S(1)}, bf16[256,1024]{1,0:T(8,128)(2,1)S(1)}, u32[]{:S(2)}, u32[]{:S(2)}) collective-permute-start(bf16[256,1024]{1,0:T(8,128)(2,1)S(1)} %get-tuple-element.85), channel_id=1, source_target_pairs={{0,1},{1,0},{2,3},{3,2},{4,5},{5,4},{6,7},{7,6},{8,9},{9,8},{10,11... | collective-permute-start | bytes 1572872 | tf_op jit(solution)/shard_map/ppermute | solution.py:755
  160.4 26.2 %collective-permute-start.22 = (bf16[64,1024]{1,0:T(8,128)(2,1)S(1)}, bf16[64,1024]{1,0:T(8,128)(2,1)S(1)}, u32[]{:S(2)}, u32[]{:S(2)}) collective-permute-start(bf16[64,1024]{1,0:T(8,128)(2,1)S(1)} %get-tuple-element.126), channel_id=1, source_target_pairs={{0,12},{4,8},{8,4},{12,0},{1,13},{5,9},{9,5},{13,1},{2,14},{6,10},... | collective-permute-start | bytes 393224 | tf_op jit(solution)/shard_map/ppermute | solution.py:843
  186.7 30.2 %collective-permute-start.55 = (bf16[512,1024]{1,0:T(8,128)(2,1)}, bf16[512,1024]{1,0:T(8,128)(2,1)}, u32[]{:S(2)}, u32[]{:S(2)}) collective-permute-start(bf16[512,1024]{1,0:T(8,128)(2,1)} %add_convert_fusion.6), channel_id=1, source_target_pairs={{0,4},{12,8},{1,5},{13,9},{2,6},{14,10},{3,7},{15,11},{16,20},{28,... | collective-permute-start | bytes 3145736 | tf_op jit(solution)/shard_map/ppermute | solution.py:780
  190.0 44.8 %collective-permute-start.59 = (bf16[1024,512]{1,0:T(8,128)(2,1)}, bf16[1024,512]{1,0:T(8,128)(2,1)}, u32[]{:S(2)}, u32[]{:S(2)}) collective-permute-start(bf16[1024,512]{1,0:T(8,128)(2,1)} %add_convert_fusion.3), channel_id=1, source_target_pairs={{0,4},{12,8},{1,5},{13,9},{2,6},{14,10},{3,7},{15,11},{16,20},{28,... | collective-permute-start | bytes 3145736 | tf_op jit(solution)/shard_map/ppermute | solution.py:780
  211.6 30.0 %collective-permute-start.36 = (bf16[256,1024]{1,0:T(8,128)(2,1)S(1)}, bf16[256,1024]{1,0:T(8,128)(2,1)S(1)}, u32[]{:S(2)}, u32[]{:S(2)}) collective-permute-start(bf16[256,1024]{1,0:T(8,128)(2,1)S(1)} %convolution_convert_fusion.10), channel_id=1, source_target_pairs={{0,1},{1,0},{2,3},{3,2},{4,5},{5,4},{6,7},{7,6},{8,9},{9,8},{10,11... | collective-permute-start | bytes 1572872 | tf_op jit(solution)/shard_map/ppermute | solution.py:762
  212.5 83.3 %collective-permute-start.35 = (bf16[256,1024]{1,0:T(8,128)(2,1)S(1)}, bf16[256,1024]{1,0:T(8,128)(2,1)S(1)}, u32[]{:S(2)}, u32[]{:S(2)}) collective-permute-start(bf16[256,1024]{1,0:T(8,128)(2,1)S(1)} %convolution_convert_fusion.11), channel_id=1, source_target_pairs={{0,1},{1,0},{2,3},{3,2},{4,5},{5,4},{6,7},{7,6},{8,9},{9,8},{10,11... | collective-permute-start | bytes 1572872 | tf_op jit(solution)/shard_map/ppermute | solution.py:764
  214.2 39.7 %collective-permute-start.46 = (bf16[512,768]{1,0:T(8,128)(2,1)S(1)}, bf16[512,768]{1,0:T(8,128)(2,1)S(1)}, u32[]{:S(2)}, u32[]{:S(2)}) collective-permute-start(bf16[512,768]{1,0:T(8,128)(2,1)S(1)} %convolution_convert_fusion.2), channel_id=1, source_target_pairs={{0,16},{16,0},{1,17},{17,1},{2,18},{18,2},{3,19},{19,3},{4,20},{20... | collective-permute-start | bytes 2359304 | tf_op jit(solution)/shard_map/ppermute | solution.py:774
  216.9 22.6 %collective-permute-start.50 = (bf16[256,512]{1,0:T(8,128)(2,1)S(1)}, bf16[256,512]{1,0:T(8,128)(2,1)S(1)}, u32[]{:S(2)}, u32[]{:S(2)}) collective-permute-start(bf16[256,512]{1,0:T(8,128)(2,1)S(1)} %convolution_convert_fusion.12), channel_id=1, source_target_pairs={{0,16},{16,0},{1,17},{17,1},{2,18},{18,2},{3,19},{19,3},{4,20},{20... | collective-permute-start | bytes 786440 | tf_op jit(solution)/shard_map/ppermute | solution.py:774
  234.9 73.1 %collective-permute-start.56 = (bf16[512,1024]{1,0:T(8,128)(2,1)}, bf16[512,1024]{1,0:T(8,128)(2,1)}, u32[]{:S(2)}, u32[]{:S(2)}) collective-permute-start(bf16[512,1024]{1,0:T(8,128)(2,1)} %add_convert_fusion.5), channel_id=1, source_target_pairs={{4,8},{8,4},{5,9},{9,5},{6,10},{10,6},{7,11},{11,7},{20,24},{24,20... | collective-permute-start | bytes 3145736 | tf_op jit(solution)/shard_map/ppermute | solution.py:782
  239.5 100.9 %collective-permute-start.60 = (bf16[1024,512]{1,0:T(8,128)(2,1)S(1)}, bf16[1024,512]{1,0:T(8,128)(2,1)}, u32[]{:S(2)}, u32[]{:S(2)}) collective-permute-start(bf16[1024,512]{1,0:T(8,128)(2,1)S(1)} %add_convert_fusion.2), channel_id=1, source_target_pairs={{4,8},{8,4},{5,9},{9,5},{6,10},{10,6},{7,11},{11,7},{20,24},{24,20... | collective-permute-start | bytes 3145736 | tf_op jit(solution)/shard_map/ppermute | solution.py:782
  252.2 44.8 %collective-permute-start.37 = (bf16[256,1024]{1,0:T(8,128)(2,1)S(1)}, bf16[256,1024]{1,0:T(8,128)(2,1)S(1)}, u32[]{:S(2)}, u32[]{:S(2)}) collective-permute-start(bf16[256,1024]{1,0:T(8,128)(2,1)S(1)} %add_convert_fusion.10), channel_id=1, source_target_pairs={{0,2},{2,0},{1,3},{3,1},{4,6},{6,4},{5,7},{7,5},{8,10},{10,8},{9,1... | collective-permute-start | bytes 1572872 | tf_op jit(solution)/shard_map/ppermute | solution.py:763
  255.8 57.4 %collective-permute-start.47 = (bf16[512,768]{1,0:T(8,128)(2,1)S(1)}, bf16[512,768]{1,0:T(8,128)(2,1)}, u32[]{:S(2)}, u32[]{:S(2)}) collective-permute-start(bf16[512,768]{1,0:T(8,128)(2,1)S(1)} %add_convert_fusion.9), channel_id=1, source_target_pairs={{0,4},{12,8},{1,5},{13,9},{2,6},{14,10},{3,7},{15,11},{16,20},{28,... | collective-permute-start | bytes 2359304 | tf_op jit(solution)/shard_map/ppermute | solution.py:780
  295.8 47.6 %collective-permute-start.53 = (bf16[256,512]{1,0:T(8,128)(2,1)}, bf16[256,512]{1,0:T(8,128)(2,1)}, u32[]{:S(2)}, u32[]{:S(2)}) collective-permute-start(bf16[256,512]{1,0:T(8,128)(2,1)} %add_convert_fusion.12), channel_id=1, source_target_pairs={{4,0},{8,12},{5,1},{9,13},{6,2},{10,14},{7,3},{11,15},{20,16},{24,... | collective-permute-start | bytes 786440 | tf_op jit(solution)/shard_map/ppermute | solution.py:784
  306.6 57.0 %collective-permute-start.40 = (bf16[64,1024]{1,0:T(8,128)(2,1)S(1)}, bf16[64,1024]{1,0:T(8,128)(2,1)}, u32[]{:S(2)}, u32[]{:S(2)}) collective-permute-start(bf16[64,1024]{1,0:T(8,128)(2,1)S(1)} %get-tuple-element.110), channel_id=1, source_target_pairs={{0,12},{4,8},{8,4},{12,0},{1,13},{5,9},{9,5},{13,1},{2,14},{6,10},... | collective-permute-start | bytes 393224 | tf_op jit(solution)/shard_map/ppermute | solution.py:843
  311.8 63.6 %collective-permute-start.57 = (bf16[512,1024]{1,0:T(8,128)(2,1)S(1)}, bf16[512,1024]{1,0:T(8,128)(2,1)}, u32[]{:S(2)}, u32[]{:S(2)}) collective-permute-start(bf16[512,1024]{1,0:T(8,128)(2,1)S(1)} %add_convert_fusion.4), channel_id=1, source_target_pairs={{4,0},{8,12},{5,1},{9,13},{6,2},{10,14},{7,3},{11,15},{20,16},{24,... | collective-permute-start | bytes 3145736 | tf_op jit(solution)/shard_map/ppermute | solution.py:784
  313.1 25.7 %collective-permute-start.44 = (f32[16,512]{1,0:T(8,128)S(1)}, f32[16,512]{1,0:T(8,128)S(1)}, u32[]{:S(2)}, u32[]{:S(2)}) collective-permute-start(f32[16,512]{1,0:T(8,128)S(1)} %pad_maximum_fusion.14), channel_id=1, source_target_pairs={{0,4},{4,0},{8,12},{12,8},{1,5},{5,1},{9,13},{13,9},{2,6},{6,2},{1... | collective-permute-start | bytes 98312 | tf_op jit(solution)/shard_map/ppermute | solution.py:956
  338.9 32.4 %collective-permute-start.48 = (bf16[512,768]{1,0:T(8,128)(2,1)}, bf16[512,768]{1,0:T(8,128)(2,1)}, u32[]{:S(2)}, u32[]{:S(2)}) collective-permute-start(bf16[512,768]{1,0:T(8,128)(2,1)} %add_convert_fusion.8), channel_id=1, source_target_pairs={{4,8},{8,4},{5,9},{9,5},{6,10},{10,6},{7,11},{11,7},{20,24},{24,20... | collective-permute-start | bytes 2359304 | tf_op jit(solution)/shard_map/ppermute | solution.py:782
  340.4 23.3 %collective-permute-start.45 = (f32[16,512]{1,0:T(8,128)S(1)}, f32[16,512]{1,0:T(8,128)S(1)}, u32[]{:S(2)}, u32[]{:S(2)}) collective-permute-start(f32[16,512]{1,0:T(8,128)S(1)} %fusion.62), channel_id=1, source_target_pairs={{0,8},{4,12},{8,0},{12,4},{1,9},{5,13},{9,1},{13,5},{2,10},{6,14},... | collective-permute-start | bytes 98312 | tf_op jit(solution)/shard_map/ppermute | solution.py:957
  343.4 25.4 %collective-permute-start.39 = (bf16[64,1024]{1,0:T(8,128)(2,1)}, bf16[64,1024]{1,0:T(8,128)(2,1)}, u32[]{:S(2)}, u32[]{:S(2)}) collective-permute-start(bf16[64,1024]{1,0:T(8,128)(2,1)} %get-tuple-element.111), channel_id=1, source_target_pairs={{0,8},{4,12},{8,0},{12,4},{1,9},{5,13},{9,1},{13,5},{2,10},{6,14},... | collective-permute-start | bytes 393224 | tf_op jit(solution)/shard_map/ppermute | solution.py:843
  363.7 28.8 %collective-permute-start.61 = (bf16[1024,512]{1,0:T(8,128)(2,1)S(1)}, bf16[1024,512]{1,0:T(8,128)(2,1)S(1)}, u32[]{:S(2)}, u32[]{:S(2)}) collective-permute-start(bf16[1024,512]{1,0:T(8,128)(2,1)S(1)} %add_convert_fusion.1), channel_id=1, source_target_pairs={{4,0},{8,12},{5,1},{9,13},{6,2},{10,14},{7,3},{11,15},{20,16},{24,... | collective-permute-start | bytes 3145736 | tf_op jit(solution)/shard_map/ppermute | solution.py:784
  372.8 33.7 %collective-permute-start.49 = (bf16[512,768]{1,0:T(8,128)(2,1)S(1)}, bf16[512,768]{1,0:T(8,128)(2,1)S(1)}, u32[]{:S(2)}, u32[]{:S(2)}) collective-permute-start(bf16[512,768]{1,0:T(8,128)(2,1)S(1)} %add_convert_fusion.7), channel_id=1, source_target_pairs={{4,0},{8,12},{5,1},{9,13},{6,2},{10,14},{7,3},{11,15},{20,16},{24,... | collective-permute-start | bytes 2359304 | tf_op jit(solution)/shard_map/ppermute | solution.py:784
  (60 other events, 611.2 us)
where the time goes:
time: 416 us; the launch traced here: 408 us
  waiting for transfers between devices  154 us (37%)
  starting transfers between devices  116 us (28%)
  matrix products  38.6 us (9%)
  other arithmetic  36.4 us (9%)
  Pallas kernels  31.6 us (8%)
  local copies, waits for them, and re-layouts  30.1 us (7%)
    ppermute x4, starting transfers between devices, sum_chained(): edge = lax.ppermute(half, 'ctx', INWARD)  50.6 us
    ppermute x4, waiting for transfers between devices, sum_chained(): outer = lax.ppermute(total, 'ctx', OUTWARD)  26.9 us
    dot_general x21, matrix products, contract(): lax.dot_general(left, right, (((left_dim,), (right_dim,)), ((), ())), pre...  25.3 us
    ppermute x4, waiting for transfers between devices, gather_sum(): peer = lax.ppermute(bf(part_of(2) + f32(across)), 'tp', PEER)  23.3 us
    ppermute x1, waiting for transfers between devices, fast_device(): small = small + lax.ppermute(small, 'ctx', xor_pairs(ctx_count, 1))  19.9 us
    ppermute x1, waiting for transfers between devices, fast_device(): small = small + lax.ppermute(small, 'ctx', xor_pairs(ctx_count, 2))  18.7 us
    ppermute x4, waiting for transfers between devices, sum_chained(): edge = lax.ppermute(half, 'ctx', INWARD)  17.8 us
    convert_element_type x11, other arithmetic, bf(): return values.astype(jnp.bfloat16)  15.7 us
  transfers between devices with their start and end apart: 62, of which 20 were waited for; matrix products, arithmetic and copies ran while one was open for 25% of the time, Pallas kernels for 7%

commit v1 on v0

--- a/solution.py
+++ b/solution.py
@@ -420,41 +420,49 @@
     )
 
 
-def attend_kernel(query_ref, key_ref, value_ref, out_ref, lse_ref, score_ref, acc_ref):
+def attend_kernel(place_ref, query_ref, key_ref, value_ref, out_ref, lse_ref, score_ref, acc_ref):
     block = pl.program_id(0)
+    place = place_ref[0]
     query = merged(query_ref[:, 0])
     rows, width = query.shape
     heads = width // HD
     scale = HD ** (-0.5)
 
     def score(other, top):
-        values = contract(stack_heads(merged(key_ref[:, other])), query, 1, 1)
+        values = contract(stack_heads(merged(key_ref[:, other ^ place])), query, 1, 1)
         values = values.reshape(heads, rows, rows)
         score_ref[other] = values
         return jnp.maximum(top, jnp.max(values, axis=1, keepdims=True))
 
     top = lax.fori_loop(0, block + 1, score, jnp.full((heads, 1, rows), NEGATIVE, jnp.float32))
 
+    acc_ref[...] = jnp.zeros_like(acc_ref)
+
     def weigh(other, total):
         values = jnp.exp((score_ref[other] - top) * scale)
-        score_ref[other] = values
+        prob = bf(values).reshape(heads * rows, rows)
+        acc_ref[...] += contract(prob, stack_heads(merged(value_ref[:, other ^ place])), 0, 0)
         return total + jnp.sum(values, axis=1, keepdims=True)
 
     total = lax.fori_loop(0, block + 1, weigh, jnp.zeros((heads, 1, rows), jnp.float32))
     lse_ref[0] = top * scale + jnp.log(total)
     inverse = 1.0 / total
-    acc_ref[...] = jnp.zeros_like(acc_ref)
-
-    def mix(other, unused):
-        prob = bf(score_ref[other] * inverse).reshape(heads * rows, rows)
-        acc_ref[...] += contract(prob, stack_heads(merged(value_ref[:, other])), 0, 0)
-        return unused
-
-    lax.fori_loop(0, block + 1, mix, 0)
-    out_ref[:, 0] = bf(acc_ref[...]).reshape(out_ref.shape[0], out_ref.shape[2], width)
+    lane = lax.broadcasted_iota(jnp.int32, (rows, 2 * HD), 1)
+    columns = [
+        jnp.transpose(jnp.broadcast_to(inverse[head], (2 * HD, rows))) for head in range(heads)
+    ]
+    factor = jnp.concatenate(
+        [
+            jnp.where(lane < HD, columns[head], columns[head + 1])
+            for head in range(0, heads, 2)
+        ],
+        axis=1,
+    )
+    out_ref[:, 0] = bf(acc_ref[...] * factor).reshape(out_ref.shape[0], out_ref.shape[2], width)
 
 
 def attend_back_kernel(
+    place_ref,
     query_ref,
     key_ref,
     value_ref,
@@ -469,6 +477,7 @@
     grad_stack,
 ):
     block = pl.program_id(0)
+    place = place_ref[0]
     blocks = pl.num_programs(0)
     query = merged(query_ref[:, 0])
     grad = merged(grad_ref[:, 0])
@@ -493,9 +502,9 @@
         value_acc[...] = jnp.zeros_like(value_acc)
 
     def one_block(other, unused):
-        key = merged(key_ref[:, other])
+        key = merged(key_ref[:, other ^ place])
         scores = contract(key, query_stack[...], 1, 1)
-        prob_grad = contract(merged(value_ref[:, other]), grad_stack[...], 1, 1)
+        prob_grad = contract(merged(value_ref[:, other ^ place]), grad_stack[...], 1, 1)
         prob = jnp.exp(scores * scale - lse)
         score_grad = bf(prob * (prob_grad - delta))
         value_acc[other] += contract(bf(prob), grad_stack[...], 1, 0)
@@ -509,46 +518,49 @@
     lax.fori_loop(0, block + 1, one_block, 0)
     slots, _, part, _ = qkv_grad_ref.shape
 
-    def place(which, other, values):
-        qkv_grad_ref[:, other, :, which * width : (which + 1) * width] = bf(values).reshape(
+    def store(which, other, values):
+        qkv_grad_ref[:, other ^ place, :, which * width : (which + 1) * width] = bf(values).reshape(
             slots, part, width
         )
 
-    place(0, block, query_acc[...] * scale)
+    store(0, block, query_acc[...] * scale)
 
     @pl.when(block == blocks - 1)
     def finish():
         for other in range(key_acc.shape[0]):
-            place(1, other, key_acc[other] * scale)
-            place(2, other, value_acc[other])
+            store(1, other, key_acc[other] * scale)
+            store(2, other, value_acc[other])
 
 
 def attend_specs(qkv):
     slots, blocks, part, width = qkv.shape
     width //= 3
-    one = pl.BlockSpec((slots, 1, part, width), lambda i: (0, i, 0, 0))
-    key = pl.BlockSpec((slots, blocks, part, width), lambda i: (0, 0, 0, 1))
-    value = pl.BlockSpec((slots, blocks, part, width), lambda i: (0, 0, 0, 2))
+    one = pl.BlockSpec((slots, 1, part, width), lambda i, place: (0, i ^ place[0], 0, 0))
+    key = pl.BlockSpec((slots, blocks, part, width), lambda i, place: (0, 0, 0, 1))
+    value = pl.BlockSpec((slots, blocks, part, width), lambda i, place: (0, 0, 0, 2))
     return slots, blocks, part, width, one, key, value
 
 
-def attend(qkv):
+def attend(place, qkv):
     slots, blocks, part, width, one, key, value = attend_specs(qkv)
     rows = slots * part
     heads = width // HD
     pairs = blocks * (blocks + 1) // 2 * heads
     return pl.pallas_call(
         attend_kernel,
-        grid=(blocks,),
-        in_specs=[one, key, value],
-        out_specs=[one, pl.BlockSpec((1, heads, 1, rows), lambda i: (i, 0, 0, 0))],
+        grid_spec=pltpu.PrefetchScalarGridSpec(
+            num_scalar_prefetch=1,
+            grid=(blocks,),
+            in_specs=[one, key, value],
+            out_specs=[one, pl.BlockSpec((1, heads, 1, rows), lambda i, place: (i, 0, 0, 0))],
+            scratch_shapes=[
+            pltpu.VMEM((blocks, heads, rows, rows), jnp.float32),
+            pltpu.VMEM((rows, width), jnp.float32),
+        ],
+        ),
         out_shape=[
             jax.ShapeDtypeStruct((slots, blocks, part, width), jnp.bfloat16),
             jax.ShapeDtypeStruct((blocks, heads, 1, rows), jnp.float32),
-        ],
-        scratch_shapes=[
-            pltpu.VMEM((blocks, heads, rows, rows), jnp.float32),
-            pltpu.VMEM((rows, width), jnp.float32),
         ],
         cost_estimate=pl.CostEstimate(
             flops=pairs * 4 * rows * rows * width,
@@ -556,41 +568,44 @@
             transcendentals=pairs * rows * rows,
         ),
         name="attend",
-    )(qkv, qkv, qkv)
-
-
-def attend_back(qkv, out, grad, lse):
+    )(place, qkv, qkv, qkv)
+
+
+def attend_back(place, qkv, out, grad, lse):
     slots, blocks, part, width, one, key, value = attend_specs(qkv)
     rows = slots * part
     heads = width // HD
     pairs = blocks * (blocks + 1) // 2 * heads
     return pl.pallas_call(
         attend_back_kernel,
-        grid=(blocks,),
-        in_specs=[
+        grid_spec=pltpu.PrefetchScalarGridSpec(
+            num_scalar_prefetch=1,
+            grid=(blocks,),
+            in_specs=[
             one,
             key,
             value,
             one,
             one,
-            pl.BlockSpec((1, heads, 1, rows), lambda i: (i, 0, 0, 0)),
+            pl.BlockSpec((1, heads, 1, rows), lambda i, place: (i, 0, 0, 0)),
         ],
-        out_specs=pl.BlockSpec(qkv.shape, lambda i: (0, 0, 0, 0)),
-        out_shape=jax.ShapeDtypeStruct(qkv.shape, jnp.bfloat16),
-        scratch_shapes=[
+            out_specs=pl.BlockSpec(qkv.shape, lambda i, place: (0, 0, 0, 0)),
+            scratch_shapes=[
             pltpu.VMEM((rows, width), jnp.float32),
             pltpu.VMEM((blocks, rows, width), jnp.float32),
             pltpu.VMEM((blocks, rows, width), jnp.float32),
             pltpu.VMEM((heads * rows, width), jnp.bfloat16),
             pltpu.VMEM((heads * rows, width), jnp.bfloat16),
         ],
+        ),
+        out_shape=jax.ShapeDtypeStruct(qkv.shape, jnp.bfloat16),
         cost_estimate=pl.CostEstimate(
             flops=pairs * 10 * rows * rows * width,
             bytes_accessed=16 * qkv.size // 3,
             transcendentals=pairs * rows * rows,
         ),
         name="attend_back",
-    )(qkv, qkv, qkv, out, grad, lse)
+    )(place, qkv, qkv, qkv, out, grad, lse)
 
 
 def unit_mask(rows, width, start):
@@ -634,11 +649,13 @@
     return jnp.where(flag == 0, own, other), jnp.where(flag == 0, other, own)
 
 
-def unpack_params_kernel(flag_ref, own_ref, other_ref, vector_ref, qkv_ref, fc_ref):
+def unpack_params_kernel(flag_ref, own_ref, other_ref, *refs):
+    vectors, qkv_ref, fc_ref = refs[:6], *refs[6:]
     flag = flag_ref[0]
     own = f32(own_ref[...])
     other = f32(other_ref[...])
-    vector_ref[...] = jnp.concatenate([own[:8], other[:8]], axis=1)
+    for row, vector in enumerate(vectors):
+        vector[...] = jnp.concatenate([own[row : row + 1], other[row : row + 1]], axis=1)
     part = HD // 2
 
     def spread(width, column):
@@ -669,8 +686,8 @@
     return pl.pallas_call(
         unpack_params_kernel,
         in_specs=[pl.BlockSpec(memory_space=pltpu.SMEM), whole, whole],
-        out_shape=[
-            jax.ShapeDtypeStruct((8, 2 * own.shape[1]), jnp.float32),
+        out_shape=[jax.ShapeDtypeStruct((1, 2 * own.shape[1]), jnp.float32)] * 6
+        + [
             jax.ShapeDtypeStruct((1, qkv_width), jnp.float32),
             jax.ShapeDtypeStruct((1, fc_width), jnp.float32),
         ],
@@ -811,6 +828,7 @@
     place_f = lax.axis_index("fsdp")
     place_c = lax.axis_index("ctx")
     place_t = lax.axis_index("tp")
+    place = place_c.astype(jnp.int32).reshape(1)
     half = width // 2
     lower = place_f == 0
 
@@ -827,18 +845,13 @@
             if step:
                 piece = lax.ppermute(piece, "ctx", xor_pairs(ctx_count, step))
             got.append(piece)
-        stacked = jnp.stack(got)
-        ordered = [
-            lax.dynamic_index_in_dim(stacked, place_c ^ step, 0, keepdims=False)
-            for step in range(ctx_count)
-        ]
-        return jnp.concatenate(ordered, axis=0)
+        return jnp.concatenate(got, axis=0)
 
     def to_positions(values):
-        mine = own_first(values).reshape(ctx_count, share_rows, width)
+        mine = own_first(values)
         got = []
         for step in range(ctx_count):
-            piece = lax.dynamic_index_in_dim(mine, place_c ^ step, 0, keepdims=False)
+            piece = mine[step * share_rows : (step + 1) * share_rows]
             if step:
                 piece = lax.ppermute(piece, "ctx", xor_pairs(ctx_count, step))
             got.append(piece)
@@ -861,6 +874,7 @@
     fc_other = lax.ppermute(fc_weight, "fsdp", SWAP)
     fc2_other = lax.ppermute(fc2_weight, "fsdp", SWAP)
     proj_full = jnp.concatenate([proj_weight, proj_other], axis=1)
+    fc_weight, fc2_weight, fc2_other = lax.optimization_barrier((fc_weight, fc2_weight, fc2_other))
     fc_full = jnp.concatenate([fc_weight, fc_other], axis=0)
     fc2_full = jnp.concatenate([fc2_weight, fc2_other], axis=1)
     qkv_full = jnp.concatenate(
@@ -872,17 +886,16 @@
     )
 
     head_width = qkv_weight.shape[2]
-    vectors, bias_qkv, bias_row = unpack_params(
-        flag, small_own, small_other, 3 * head_width, fc_weight.shape[1]
-    )
-    gain_one, shift_one, bias_proj, gain_two, shift_two, bias_fc2 = (vectors[n] for n in range(6))
+    gain_one, shift_one, bias_proj, gain_two, shift_two, bias_fc2, bias_qkv, bias_row = (
+        unpack_params(flag, small_own, small_other, 3 * head_width, fc_weight.shape[1])
+    )
 
     first_f, normed_one, spread_one = norm_forward(flat, gain_one, shift_one)
     first_in = join_rows(spread_parts(bf(first_f)))
     head_shape = (tp_count, ctx_count, share_rows, head_width)
     qkv = bf(matmul(first_in, qkv_full) + bias_qkv)
     qkv = qkv.reshape(head_shape[:3] + (3 * head_width,))
-    attended_four, lse = attend(qkv)
+    attended_four, lse = attend(place, qkv)
     attended = attended_four.reshape(-1, head_width)
 
     def rows_of(values, slot):
@@ -926,7 +939,7 @@
 
     branch = join_rows(branch)
     attended_grad = bf(contract(branch, proj_full, 1, 1)).reshape(head_shape)
-    qkv_grad = attend_back(qkv, attended_four, attended_grad, lse).reshape(-1, 3 * head_width)
+    qkv_grad = attend_back(place, qkv, attended_four, attended_grad, lse).reshape(-1, 3 * head_width)
     grad_proj = sum_chained(lambda which: contract(attended, halved(branch, which), 0, 0))
     grad_qkv = sum_chained(lambda which: contract(halved(first_in, which), qkv_grad, 0, 0))
     grad_qkv = jnp.stack(

time: 416 us -> 428 us (1.029)
  waiting for transfers between devices: 154 us -> 173 us
  local copies, waits for them, and re-layouts: 30.1 us -> 21.8 us
    ppermute x1, waiting for transfers between devices: 0.01 us -> 12.6 us  [fast_device(): fc2_other = lax.ppermute(fc2_weight, 'fsdp', SWAP)]
    ppermute x6, starting transfers between devices: 9.74 us -> 16.7 us  [to_sequences(): piece = lax.ppermute(piece, 'ctx', xor_pairs(ctx_count, step))]
    unnamed x75 -> x81, local copies, waits for them, and re-layouts: 13.7 us -> 11.9 us
  transfers between devices with their start and end apart: 62 -> 62, of which waited for: 20 -> 21; matrix products, arithmetic and copies ran while one was open for 25% -> 22% of each run, Pallas kernels for 7% -> 7%
where the time goes in v1:
time: 428 us; the launch traced here: 421 us
  waiting for transfers between devices  173 us (40%)
  starting transfers between devices  118 us (28%)
  matrix products  39.4 us (9%)
  other arithmetic  34.7 us (8%)
  Pallas kernels  31.8 us (7%)
  local copies, waits for them, and re-layouts  21.8 us (5%)
    ppermute x4, starting transfers between devices, sum_chained(): edge = lax.ppermute(half, 'ctx', INWARD)  49.1 us
    ppermute x4, waiting for transfers between devices, sum_chained(): outer = lax.ppermute(total, 'ctx', OUTWARD)  26.9 us
    dot_general x21, matrix products, contract(): lax.dot_general(left, right, (((left_dim,), (right_dim,)), ((), ())), pre...  26.2 us
    ppermute x4, waiting for transfers between devices, gather_sum(): peer = lax.ppermute(bf(part_of(2) + f32(across)), 'tp', PEER)  23.8 us
    ppermute x1, waiting for transfers between devices, fast_device(): small = small + lax.ppermute(small, 'ctx', xor_pairs(ctx_count, 1))  19.4 us
    ppermute x4, waiting for transfers between devices, sum_chained(): edge = lax.ppermute(half, 'ctx', INWARD)  18.6 us
    ppermute x1, waiting for transfers between devices, fast_device(): small = small + lax.ppermute(small, 'ctx', xor_pairs(ctx_count, 2))  18.5 us
    ppermute x1, waiting for transfers between devices, fast_device(): proj_other = lax.ppermute(proj_weight, 'fsdp', SWAP)  18 us
  transfers between devices with their start and end apart: 62, of which 21 were waited for; matrix products, arithmetic and copies ran while one was open for 22% of the time, Pallas kernels for 7%

profile of v1, /device:TPU:0, one launch (start us, length us, event | category | flops | bytes accessed | tf_op | source)
XLA Modules:
  0.0 420.8 jit_solution(9180346322715353781)
XLA Ops:
  2.1 3.0 collective-permute-start.3
  7.9 3.6 collective-permute-start.2
  13.8 3.4 collective-permute-start.23
  18.0 3.0 collective-permute-done.25
  20.9 8.7 %collective-permute-start = (bf16[64,1024]{1,0:T(8,128)(2,1)}, bf16[64,1024]{1,0:T(8,128)(2,1)S(1)}, u32[]{:S(2)}, u32[]{:S(2)}) collective-permute-start(bf16[64,1024]{1,0:T(8,128)(2,1)} %get-tuple-element.147), channel_id=1, source_target_pairs={{0,4},{4,0},{8,12},{12,8},{1,5},{5,1},{9,13},{13,9},{2,6},{6,2},{1... | collective-permute-start | bytes 393224 | tf_op jit(solution)/shard_map/ppermute | solution.py:846
  40.7 18.0 %collective-permute-done.8 = bf16[256,512]{1,0:T(8,128)(2,1)S(1)} collective-permute-done((bf16[256,512]{1,0:T(8,128)(2,1)}, bf16[256,512]{1,0:T(8,128)(2,1)S(1)}, u32[]{:S(2)}, u32[]{:S(2)}) %collective-permute-start.8) | collective-permute-done | bytes 262176 | tf_op jit(solution)/shard_map/ppermute | solution.py:873
  65.0 3.0 collective-permute-done.5
  68.7 12.6 %collective-permute-done.12 = bf16[1024,512]{1,0:T(8,128)(2,1)S(1)} collective-permute-done((bf16[1024,512]{1,0:T(8,128)(2,1)S(1)}, bf16[1024,512]{1,0:T(8,128)(2,1)S(1)}, u32[]{:S(2)}, u32[]{:S(2)}) %collective-permute-start.12) | collective-permute-done | bytes 1048608 | tf_op jit(solution)/shard_map/ppermute | solution.py:875
  83.2 2.8 fusion.76
  86.7 2.9 add_convert_fusion
  89.6 11.5 %attend.1 = (bf16[4,4,64,256]{3,2,1,0:T(8,128)(2,1)}, f32[4,4,1,256]{3,2,1,0:T(1,128)}) custom-call(s32[1]{0:T(128)} %bitcast.4.place_ref, bf16[4,4,64,768]{3,2,1,0:T(8,128)(2,1)} %bitcast.173, bf16[4,4,64,768]{3,2,1,0:T(8,128)(2,1)} %bitcast.174, bf16[4,4,64,768]{3,2,1,0:T(8,128)(2,1)} %bitcast.175), custom_call_target="tpu_custom_call" | custom-call | flops 2684354560 | bytes 2097152 | tf_op jit(solution)/shard_map/attend/pallas_call | solution.py:549
  111.0 8.0 %collective-permute-done.11 = bf16[256,1024]{1,0:T(8,128)(2,1)S(1)} collective-permute-done((bf16[256,1024]{1,0:T(8,128)(2,1)S(1)}, bf16[256,1024]{1,0:T(8,128)(2,1)S(1)}, u32[]{:S(2)}, u32[]{:S(2)}) %collective-permute-start.11) | collective-permute-done | bytes 524320 | tf_op jit(solution)/shard_map/ppermute | solution.py:780
  127.1 8.6 %collective-permute-done.16 = bf16[256,1024]{1,0:T(8,128)(2,1)S(1)} collective-permute-done((bf16[256,1024]{1,0:T(8,128)(2,1)S(1)}, bf16[256,1024]{1,0:T(8,128)(2,1)S(1)}, u32[]{:S(2)}, u32[]{:S(2)}) %collective-permute-start.16) | collective-permute-done | bytes 524320 | tf_op jit(solution)/shard_map/ppermute | solution.py:773
  151.7 9.9 %collective-permute-done.31 = bf16[256,1024]{1,0:T(8,128)(2,1)S(1)} collective-permute-done((bf16[256,1024]{1,0:T(8,128)(2,1)S(1)}, bf16[256,1024]{1,0:T(8,128)(2,1)S(1)}, u32[]{:S(2)}, u32[]{:S(2)}) %collective-permute-start.31) | collective-permute-done | bytes 524320 | tf_op jit(solution)/shard_map/ppermute | solution.py:780
  166.9 6.0 %collective-permute-done.19 = bf16[256,1024]{1,0:T(8,128)(2,1)S(1)} collective-permute-done((bf16[256,1024]{1,0:T(8,128)(2,1)S(1)}, bf16[256,1024]{1,0:T(8,128)(2,1)S(1)}, u32[]{:S(2)}, u32[]{:S(2)}) %collective-permute-start.19) | collective-permute-done | bytes 524320 | tf_op jit(solution)/shard_map/ppermute | solution.py:780
  173.9 3.0 collective-permute-start.22
  177.0 14.6 %collective-permute-done.58 = bf16[1024,512]{1,0:T(8,128)(2,1)S(1)} collective-permute-done((bf16[1024,512]{1,0:T(8,128)(2,1)S(1)}, bf16[1024,512]{1,0:T(8,128)(2,1)S(1)}, u32[]{:S(2)}, u32[]{:S(2)}) %collective-permute-start.58) | collective-permute-done | bytes 1048608 | tf_op jit(solution)/shard_map/ppermute | solution.py:791
  193.0 2.3 add_convert_fusion.3
  199.6 3.0 collective-permute-start.55
  202.7 2.3 collective-permute-start.59
  208.1 13.9 %attend_back.1 = bf16[4,4,64,768]{3,2,1,0:T(8,128)(2,1)} custom-call(s32[1]{0:T(128)} %bitcast.4.place_ref, bf16[4,4,64,768]{3,2,1,0:T(8,128)(2,1)} %bitcast.176, bf16[4,4,64,768]{3,2,1,0:T(8,128)(2,1)} %bitcast.177, bf16[4,4,64,768]{3,2,1,0:T(8,128)(2,1)} %bitcast.178, bf16[4,4,64,256]{3,2,1,0:T(8,128)(2,1)} %get-tuple-element.40.out_ref, ...), custom_call_target="tpu_custom_call" | custom-call | flops 6710886400 | bytes 4194304 | tf_op jit(solution)/shard_map/attend_back/pallas_call | solution.py:579
  233.0 14.4 %collective-permute-done.59 = bf16[1024,512]{1,0:T(8,128)(2,1)} collective-permute-done((bf16[1024,512]{1,0:T(8,128)(2,1)}, bf16[1024,512]{1,0:T(8,128)(2,1)}, u32[]{:S(2)}, u32[]{:S(2)}) %collective-permute-start.59) | collective-permute-done | bytes 1048608 | tf_op jit(solution)/shard_map/ppermute | solution.py:797
  254.4 5.6 %collective-permute-start.51 = (bf16[256,512]{1,0:T(8,128)(2,1)S(1)}, bf16[256,512]{1,0:T(8,128)(2,1)S(1)}, u32[]{:S(2)}, u32[]{:S(2)}) collective-permute-start(bf16[256,512]{1,0:T(8,128)(2,1)S(1)} %fusion.16), channel_id=1, source_target_pairs={{0,4},{12,8},{1,5},{13,9},{2,6},{14,10},{3,7},{15,11},{16,20},{28,... | collective-permute-start | bytes 786440 | tf_op jit(solution)/shard_map/ppermute | solution.py:797
  260.6 4.2 collective-permute-done.51
  269.2 38.2 %collective-permute-start.47 = (bf16[512,768]{1,0:T(8,128)(2,1)}, bf16[512,768]{1,0:T(8,128)(2,1)}, u32[]{:S(2)}, u32[]{:S(2)}) collective-permute-start(bf16[512,768]{1,0:T(8,128)(2,1)} %add_convert_fusion.9), channel_id=1, source_target_pairs={{0,4},{12,8},{1,5},{13,9},{2,6},{14,10},{3,7},{15,11},{16,20},{28,... | collective-permute-start | bytes 2359304 | tf_op jit(solution)/shard_map/ppermute | solution.py:797
  326.1 3.7 collective-permute-start.44
  329.8 2.4 add_convert_fusion.8
  332.2 19.4 %collective-permute-done.44 = f32[16,512]{1,0:T(8,128)S(1)} collective-permute-done((f32[16,512]{1,0:T(8,128)S(1)}, f32[16,512]{1,0:T(8,128)S(1)}, u32[]{:S(2)}, u32[]{:S(2)}) %collective-permute-start.44) | collective-permute-done | bytes 32800 | tf_op jit(solution)/shard_map/ppermute | solution.py:969
  357.7 18.5 %collective-permute-done.45 = f32[16,512]{1,0:T(8,128)S(1)} collective-permute-done((f32[16,512]{1,0:T(8,128)S(1)}, f32[16,512]{1,0:T(8,128)S(1)}, u32[]{:S(2)}, u32[]{:S(2)}) %collective-permute-start.45) | collective-permute-done | bytes 32800 | tf_op jit(solution)/shard_map/ppermute | solution.py:970
  388.0 2.7 select_convert_fusion.1
  390.7 14.5 %collective-permute-done.61 = bf16[1024,512]{1,0:T(8,128)(2,1)S(1)} collective-permute-done((bf16[1024,512]{1,0:T(8,128)(2,1)S(1)}, bf16[1024,512]{1,0:T(8,128)(2,1)S(1)}, u32[]{:S(2)}, u32[]{:S(2)}) %collective-permute-start.61) | collective-permute-done | bytes 1048608 | tf_op jit(solution)/shard_map/ppermute | solution.py:801
  406.7 12.3 %collective-permute-done.49 = bf16[512,768]{1,0:T(8,128)(2,1)S(1)} collective-permute-done((bf16[512,768]{1,0:T(8,128)(2,1)S(1)}, bf16[512,768]{1,0:T(8,128)(2,1)S(1)}, u32[]{:S(2)}, u32[]{:S(2)}) %collective-permute-start.49) | collective-permute-done | bytes 786464 | tf_op jit(solution)/shard_map/ppermute | solution.py:801
  (287 shorter events, 139.0 us)
Async XLA Ops:
  7.9 28.4 %collective-permute-start.2 = (bf16[64,1024]{1,0:T(8,128)(2,1)}, bf16[64,1024]{1,0:T(8,128)(2,1)S(1)}, u32[]{:S(2)}, u32[]{:S(2)}) collective-permute-start(bf16[64,1024]{1,0:T(8,128)(2,1)} %get-tuple-element.145), channel_id=1, source_target_pairs={{0,12},{4,8},{8,4},{12,0},{1,13},{5,9},{9,5},{13,1},{2,14},{6,10},... | collective-permute-start | bytes 393224 | tf_op jit(solution)/shard_map/ppermute | solution.py:846
  32.5 35.4 %collective-permute-start.7 = (bf16[3,512,256]{2,1,0:T(8,128)(2,1)}, bf16[3,512,256]{2,1,0:T(8,128)(2,1)S(1)}, u32[]{:S(2)}, u32[]{:S(2)}) collective-permute-start(bf16[3,512,256]{2,1,0:T(8,128)(2,1)} %param.18), channel_id=1, source_target_pairs={{0,16},{16,0},{1,17},{17,1},{2,18},{18,2},{3,19},{19,3},{4,20},{20... | collective-permute-start | bytes 2359304 | tf_op jit(solution)/shard_map/ppermute | solution.py:872
  33.1 25.7 %collective-permute-start.8 = (bf16[256,512]{1,0:T(8,128)(2,1)}, bf16[256,512]{1,0:T(8,128)(2,1)S(1)}, u32[]{:S(2)}, u32[]{:S(2)}) collective-permute-start(bf16[256,512]{1,0:T(8,128)(2,1)} %param.20), channel_id=1, source_target_pairs={{0,16},{16,0},{1,17},{17,1},{2,18},{18,2},{3,19},{19,3},{4,20},{20... | collective-permute-start | bytes 786440 | tf_op jit(solution)/shard_map/ppermute | solution.py:873
  36.3 44.9 %collective-permute-start.12 = (bf16[1024,512]{1,0:T(8,128)(2,1)S(1)}, bf16[1024,512]{1,0:T(8,128)(2,1)S(1)}, u32[]{:S(2)}, u32[]{:S(2)}) collective-permute-start(bf16[1024,512]{1,0:T(8,128)(2,1)S(1)} %copy-done.15), channel_id=1, source_target_pairs={{0,16},{16,0},{1,17},{17,1},{2,18},{18,2},{3,19},{19,3},{4,20},{20... | collective-permute-start | bytes 3145736 | tf_op jit(solution)/shard_map/ppermute | solution.py:875
  36.9 26.2 %collective-permute-start.28 = (bf16[256,1024]{1,0:T(8,128)(2,1)S(1)}, bf16[256,1024]{1,0:T(8,128)(2,1)}, u32[]{:S(2)}, u32[]{:S(2)}) collective-permute-start(bf16[256,1024]{1,0:T(8,128)(2,1)S(1)} %get-tuple-element.93), channel_id=1, source_target_pairs={{0,2},{2,0},{1,3},{3,1},{4,6},{6,4},{5,7},{7,5},{8,10},{10,8},{9,1... | collective-permute-start | bytes 1572872 | tf_op jit(solution)/shard_map/ppermute | solution.py:773
  38.4 23.2 %collective-permute-start.26 = (bf16[256,1024]{1,0:T(8,128)(2,1)S(1)}, bf16[256,1024]{1,0:T(8,128)(2,1)S(1)}, u32[]{:S(2)}, u32[]{:S(2)}) collective-permute-start(bf16[256,1024]{1,0:T(8,128)(2,1)S(1)} %get-tuple-element.93), channel_id=1, source_target_pairs={{0,1},{1,0},{2,3},{3,2},{4,5},{5,4},{6,7},{7,6},{8,9},{9,8},{10,11... | collective-permute-start | bytes 1572872 | tf_op jit(solution)/shard_map/ppermute | solution.py:772
  61.7 46.2 %collective-permute-start.13 = (bf16[512,1024]{1,0:T(8,128)(2,1)}, bf16[512,1024]{1,0:T(8,128)(2,1)}, u32[]{:S(2)}, u32[]{:S(2)}) collective-permute-start(bf16[512,1024]{1,0:T(8,128)(2,1)} %param.24), channel_id=1, source_target_pairs={{0,16},{16,0},{1,17},{17,1},{2,18},{18,2},{3,19},{19,3},{4,20},{20... | collective-permute-start | bytes 3145736 | tf_op jit(solution)/shard_map/ppermute | solution.py:874
  67.9 41.2 %collective-permute-start.29 = (bf16[256,1024]{1,0:T(8,128)(2,1)}, bf16[256,1024]{1,0:T(8,128)(2,1)}, u32[]{:S(2)}, u32[]{:S(2)}) collective-permute-start(bf16[256,1024]{1,0:T(8,128)(2,1)} %collective-permute-done.28), channel_id=1, source_target_pairs={{0,1},{1,0},{2,3},{3,2},{4,5},{5,4},{6,7},{7,6},{8,9},{9,8},{10,11... | collective-permute-start | bytes 1572872 | tf_op jit(solution)/shard_map/ppermute | solution.py:774
  127.0 39.9 %collective-permute-start.15 = (bf16[256,1024]{1,0:T(8,128)(2,1)S(1)}, bf16[256,1024]{1,0:T(8,128)(2,1)S(1)}, u32[]{:S(2)}, u32[]{:S(2)}) collective-permute-start(bf16[256,1024]{1,0:T(8,128)(2,1)S(1)} %convolution_convert_fusion.9), channel_id=1, source_target_pairs={{0,1},{1,0},{2,3},{3,2},{4,5},{5,4},{6,7},{7,6},{8,9},{9,8},{10,11... | collective-permute-start | bytes 1572872 | tf_op jit(solution)/shard_map/ppermute | solution.py:781
  143.9 51.4 %collective-permute-start.54 = (bf16[512,1024]{1,0:T(8,128)(2,1)S(1)}, bf16[512,1024]{1,0:T(8,128)(2,1)S(1)}, u32[]{:S(2)}, u32[]{:S(2)}) collective-permute-start(bf16[512,1024]{1,0:T(8,128)(2,1)S(1)} %convolution_convert_fusion.1), channel_id=1, source_target_pairs={{0,16},{16,0},{1,17},{17,1},{2,18},{18,2},{3,19},{19,3},{4,20},{20... | collective-permute-start | bytes 3145736 | tf_op jit(solution)/shard_map/ppermute | solution.py:791
  148.9 42.6 %collective-permute-start.58 = (bf16[1024,512]{1,0:T(8,128)(2,1)S(1)}, bf16[1024,512]{1,0:T(8,128)(2,1)S(1)}, u32[]{:S(2)}, u32[]{:S(2)}) collective-permute-start(bf16[1024,512]{1,0:T(8,128)(2,1)S(1)} %convolution_convert_fusion), channel_id=1, source_target_pairs={{0,16},{16,0},{1,17},{17,1},{2,18},{18,2},{3,19},{19,3},{4,20},{20... | collective-permute-start | bytes 3145736 | tf_op jit(solution)/shard_map/ppermute | solution.py:791
  165.4 32.0 %collective-permute-start.33 = (bf16[256,1024]{1,0:T(8,128)(2,1)S(1)}, bf16[256,1024]{1,0:T(8,128)(2,1)S(1)}, u32[]{:S(2)}, u32[]{:S(2)}) collective-permute-start(bf16[256,1024]{1,0:T(8,128)(2,1)S(1)} %get-tuple-element.95), channel_id=1, source_target_pairs={{0,2},{2,0},{1,3},{3,1},{4,6},{6,4},{5,7},{7,5},{8,10},{10,8},{9,1... | collective-permute-start | bytes 1572872 | tf_op jit(solution)/shard_map/ppermute | solution.py:773
  166.9 39.5 %collective-permute-start.32 = (bf16[256,1024]{1,0:T(8,128)(2,1)S(1)}, bf16[256,1024]{1,0:T(8,128)(2,1)S(1)}, u32[]{:S(2)}, u32[]{:S(2)}) collective-permute-start(bf16[256,1024]{1,0:T(8,128)(2,1)S(1)} %get-tuple-element.95), channel_id=1, source_target_pairs={{0,1},{1,0},{2,3},{3,2},{4,5},{5,4},{6,7},{7,6},{8,9},{9,8},{10,11... | collective-permute-start | bytes 1572872 | tf_op jit(solution)/shard_map/ppermute | solution.py:772
  173.9 25.7 %collective-permute-start.22 = (bf16[64,1024]{1,0:T(8,128)(2,1)S(1)}, bf16[64,1024]{1,0:T(8,128)(2,1)S(1)}, u32[]{:S(2)}, u32[]{:S(2)}) collective-permute-start(bf16[64,1024]{1,0:T(8,128)(2,1)S(1)} %get-tuple-element.135), channel_id=1, source_target_pairs={{0,12},{4,8},{8,4},{12,0},{1,13},{5,9},{9,5},{13,1},{2,14},{6,10},... | collective-permute-start | bytes 393224 | tf_op jit(solution)/shard_map/ppermute | solution.py:856
  199.6 29.9 %collective-permute-start.55 = (bf16[512,1024]{1,0:T(8,128)(2,1)}, bf16[512,1024]{1,0:T(8,128)(2,1)}, u32[]{:S(2)}, u32[]{:S(2)}) collective-permute-start(bf16[512,1024]{1,0:T(8,128)(2,1)} %add_convert_fusion.6), channel_id=1, source_target_pairs={{0,4},{12,8},{1,5},{13,9},{2,6},{14,10},{3,7},{15,11},{16,20},{28,... | collective-permute-start | bytes 3145736 | tf_op jit(solution)/shard_map/ppermute | solution.py:797
  202.7 44.8 %collective-permute-start.59 = (bf16[1024,512]{1,0:T(8,128)(2,1)}, bf16[1024,512]{1,0:T(8,128)(2,1)}, u32[]{:S(2)}, u32[]{:S(2)}) collective-permute-start(bf16[1024,512]{1,0:T(8,128)(2,1)} %add_convert_fusion.3), channel_id=1, source_target_pairs={{0,4},{12,8},{1,5},{13,9},{2,6},{14,10},{3,7},{15,11},{16,20},{28,... | collective-permute-start | bytes 3145736 | tf_op jit(solution)/shard_map/ppermute | solution.py:797
  224.4 30.0 %collective-permute-start.36 = (bf16[256,1024]{1,0:T(8,128)(2,1)S(1)}, bf16[256,1024]{1,0:T(8,128)(2,1)S(1)}, u32[]{:S(2)}, u32[]{:S(2)}) collective-permute-start(bf16[256,1024]{1,0:T(8,128)(2,1)S(1)} %convolution_convert_fusion.10), channel_id=1, source_target_pairs={{0,1},{1,0},{2,3},{3,2},{4,5},{5,4},{6,7},{7,6},{8,9},{9,8},{10,11... | collective-permute-start | bytes 1572872 | tf_op jit(solution)/shard_map/ppermute | solution.py:779
  225.3 82.8 %collective-permute-start.35 = (bf16[256,1024]{1,0:T(8,128)(2,1)S(1)}, bf16[256,1024]{1,0:T(8,128)(2,1)S(1)}, u32[]{:S(2)}, u32[]{:S(2)}) collective-permute-start(bf16[256,1024]{1,0:T(8,128)(2,1)S(1)} %convolution_convert_fusion.11), channel_id=1, source_target_pairs={{0,1},{1,0},{2,3},{3,2},{4,5},{5,4},{6,7},{7,6},{8,9},{9,8},{10,11... | collective-permute-start | bytes 1572872 | tf_op jit(solution)/shard_map/ppermute | solution.py:781
  226.9 39.5 %collective-permute-start.46 = (bf16[512,768]{1,0:T(8,128)(2,1)S(1)}, bf16[512,768]{1,0:T(8,128)(2,1)S(1)}, u32[]{:S(2)}, u32[]{:S(2)}) collective-permute-start(bf16[512,768]{1,0:T(8,128)(2,1)S(1)} %convolution_convert_fusion.2), channel_id=1, source_target_pairs={{0,16},{16,0},{1,17},{17,1},{2,18},{18,2},{3,19},{19,3},{4,20},{20... | collective-permute-start | bytes 2359304 | tf_op jit(solution)/shard_map/ppermute | solution.py:791
  247.4 73.5 %collective-permute-start.56 = (bf16[512,1024]{1,0:T(8,128)(2,1)S(1)}, bf16[512,1024]{1,0:T(8,128)(2,1)}, u32[]{:S(2)}, u32[]{:S(2)}) collective-permute-start(bf16[512,1024]{1,0:T(8,128)(2,1)S(1)} %add_convert_fusion.5), channel_id=1, source_target_pairs={{4,8},{8,4},{5,9},{9,5},{6,10},{10,6},{7,11},{11,7},{20,24},{24,20... | collective-permute-start | bytes 3145736 | tf_op jit(solution)/shard_map/ppermute | solution.py:799
  252.3 100.9 %collective-permute-start.60 = (bf16[1024,512]{1,0:T(8,128)(2,1)S(1)}, bf16[1024,512]{1,0:T(8,128)(2,1)}, u32[]{:S(2)}, u32[]{:S(2)}) collective-permute-start(bf16[1024,512]{1,0:T(8,128)(2,1)S(1)} %add_convert_fusion.2), channel_id=1, source_target_pairs={{4,8},{8,4},{5,9},{9,5},{6,10},{10,6},{7,11},{11,7},{20,24},{24,20... | collective-permute-start | bytes 3145736 | tf_op jit(solution)/shard_map/ppermute | solution.py:799
  264.8 44.6 %collective-permute-start.37 = (bf16[256,1024]{1,0:T(8,128)(2,1)S(1)}, bf16[256,1024]{1,0:T(8,128)(2,1)S(1)}, u32[]{:S(2)}, u32[]{:S(2)}) collective-permute-start(bf16[256,1024]{1,0:T(8,128)(2,1)S(1)} %add_convert_fusion.10), channel_id=1, source_target_pairs={{0,2},{2,0},{1,3},{3,1},{4,6},{6,4},{5,7},{7,5},{8,10},{10,8},{9,1... | collective-permute-start | bytes 1572872 | tf_op jit(solution)/shard_map/ppermute | solution.py:780
  269.2 56.9 %collective-permute-start.47 = (bf16[512,768]{1,0:T(8,128)(2,1)}, bf16[512,768]{1,0:T(8,128)(2,1)}, u32[]{:S(2)}, u32[]{:S(2)}) collective-permute-start(bf16[512,768]{1,0:T(8,128)(2,1)} %add_convert_fusion.9), channel_id=1, source_target_pairs={{0,4},{12,8},{1,5},{13,9},{2,6},{14,10},{3,7},{15,11},{16,20},{28,... | collective-permute-start | bytes 2359304 | tf_op jit(solution)/shard_map/ppermute | solution.py:797
  308.1 48.0 %collective-permute-start.53 = (bf16[256,512]{1,0:T(8,128)(2,1)}, bf16[256,512]{1,0:T(8,128)(2,1)}, u32[]{:S(2)}, u32[]{:S(2)}) collective-permute-start(bf16[256,512]{1,0:T(8,128)(2,1)} %add_convert_fusion.12), channel_id=1, source_target_pairs={{4,0},{8,12},{5,1},{9,13},{6,2},{10,14},{7,3},{11,15},{20,16},{24,... | collective-permute-start | bytes 786440 | tf_op jit(solution)/shard_map/ppermute | solution.py:801
  319.6 56.7 %collective-permute-start.40 = (bf16[64,1024]{1,0:T(8,128)(2,1)S(1)}, bf16[64,1024]{1,0:T(8,128)(2,1)}, u32[]{:S(2)}, u32[]{:S(2)}) collective-permute-start(bf16[64,1024]{1,0:T(8,128)(2,1)S(1)} %get-tuple-element.120), channel_id=1, source_target_pairs={{0,12},{4,8},{8,4},{12,0},{1,13},{5,9},{9,5},{13,1},{2,14},{6,10},... | collective-permute-start | bytes 393224 | tf_op jit(solution)/shard_map/ppermute | solution.py:856
  324.8 63.3 %collective-permute-start.57 = (bf16[512,1024]{1,0:T(8,128)(2,1)S(1)}, bf16[512,1024]{1,0:T(8,128)(2,1)}, u32[]{:S(2)}, u32[]{:S(2)}) collective-permute-start(bf16[512,1024]{1,0:T(8,128)(2,1)S(1)} %add_convert_fusion.4), channel_id=1, source_target_pairs={{4,0},{8,12},{5,1},{9,13},{6,2},{10,14},{7,3},{11,15},{20,16},{24,... | collective-permute-start | bytes 3145736 | tf_op jit(solution)/shard_map/ppermute | solution.py:801
  326.1 25.5 %collective-permute-start.44 = (f32[16,512]{1,0:T(8,128)S(1)}, f32[16,512]{1,0:T(8,128)S(1)}, u32[]{:S(2)}, u32[]{:S(2)}) collective-permute-start(f32[16,512]{1,0:T(8,128)S(1)} %pad_maximum_fusion.12), channel_id=1, source_target_pairs={{0,4},{4,0},{8,12},{12,8},{1,5},{5,1},{9,13},{13,9},{2,6},{6,2},{1... | collective-permute-start | bytes 98312 | tf_op jit(solution)/shard_map/ppermute | solution.py:969
  351.6 32.2 %collective-permute-start.48 = (bf16[512,768]{1,0:T(8,128)(2,1)}, bf16[512,768]{1,0:T(8,128)(2,1)}, u32[]{:S(2)}, u32[]{:S(2)}) collective-permute-start(bf16[512,768]{1,0:T(8,128)(2,1)} %add_convert_fusion.8), channel_id=1, source_target_pairs={{4,8},{8,4},{5,9},{9,5},{6,10},{10,6},{7,11},{11,7},{20,24},{24,20... | collective-permute-start | bytes 2359304 | tf_op jit(solution)/shard_map/ppermute | solution.py:799
  353.2 23.0 %collective-permute-start.45 = (f32[16,512]{1,0:T(8,128)S(1)}, f32[16,512]{1,0:T(8,128)S(1)}, u32[]{:S(2)}, u32[]{:S(2)}) collective-permute-start(f32[16,512]{1,0:T(8,128)S(1)} %fusion.62), channel_id=1, source_target_pairs={{0,8},{4,12},{8,0},{12,4},{1,9},{5,13},{9,1},{13,5},{2,10},{6,14},... | collective-permute-start | bytes 98312 | tf_op jit(solution)/shard_map/ppermute | solution.py:970
  356.2 25.2 %collective-permute-start.39 = (bf16[64,1024]{1,0:T(8,128)(2,1)}, bf16[64,1024]{1,0:T(8,128)(2,1)S(1)}, u32[]{:S(2)}, u32[]{:S(2)}) collective-permute-start(bf16[64,1024]{1,0:T(8,128)(2,1)} %get-tuple-element.121), channel_id=1, source_target_pairs={{0,8},{4,12},{8,0},{12,4},{1,9},{5,13},{9,1},{13,5},{2,10},{6,14},... | collective-permute-start | bytes 393224 | tf_op jit(solution)/shard_map/ppermute | solution.py:856
  376.2 29.0 %collective-permute-start.61 = (bf16[1024,512]{1,0:T(8,128)(2,1)S(1)}, bf16[1024,512]{1,0:T(8,128)(2,1)S(1)}, u32[]{:S(2)}, u32[]{:S(2)}) collective-permute-start(bf16[1024,512]{1,0:T(8,128)(2,1)S(1)} %add_convert_fusion.1), channel_id=1, source_target_pairs={{4,0},{8,12},{5,1},{9,13},{6,2},{10,14},{7,3},{11,15},{20,16},{24,... | collective-permute-start | bytes 3145736 | tf_op jit(solution)/shard_map/ppermute | solution.py:801
  385.4 33.6 %collective-permute-start.49 = (bf16[512,768]{1,0:T(8,128)(2,1)S(1)}, bf16[512,768]{1,0:T(8,128)(2,1)S(1)}, u32[]{:S(2)}, u32[]{:S(2)}) collective-permute-start(bf16[512,768]{1,0:T(8,128)(2,1)S(1)} %add_convert_fusion.7), channel_id=1, source_target_pairs={{4,0},{8,12},{5,1},{9,13},{6,2},{10,14},{7,3},{11,15},{20,16},{24,... | collective-permute-start | bytes 2359304 | tf_op jit(solution)/shard_map/ppermute | solution.py:801
  (63 other events, 704.4 us)
